TPU v7x, 256 devices: a whole 4x4x8 slice. The times are simulated.
256 devices in a mesh: grp: 32 (over y, x, core), own: 8 (over z).
Axes of the slice: x: 4, y: 4, z: 8, core: 2. Of those that a mesh axis runs over, the one named last changes fastest.
Arguments:
- embeddings: bfloat16 [2048, 32, 1024], P(('grp', 'own')), may hold values from -16 to 16
- cluster_ids: int32 [2048, 32], P(('grp', 'own')), may hold values from 0 to 3
- owners: int32 [2048, 1], P(('grp', 'own')), may hold values from 0 to 7; in each aligned block of 8 rows (0 to 7, 8 to 15, ...) at most 2 rows name the same one
- pattern: int32 [32, 32], replicated, may hold values 0 or 1
Outputs:
- best: float32 [2048, 32], P(('grp', 'own'))
Inputs may be any that keep to these rules, and one draw needn't show every extreme that they name: `owners`: A device sends at most 2 tiles to one owner; some device sends exactly 2 tiles to one owner.
All inputs are finite; a program needn't handle non-finite values.
Results may differ from a plain program's by a relative error of at most 0.00057.
Values may be sent and summed in bfloat16 or wider, within the bound.
No kernel may reach another device: no remote copies, remote signals or barrier semaphores. Data moves between devices by JAX's collectives and lax.ppermute only.
A program may use at most 64 MiB of HBM per device.

v0:
```python
import jax
import jax.numpy as jnp
from jax import lax
from jax.sharding import PartitionSpec as P

CAPACITY = 2


def passed_along(value, axis, steps):
    count = lax.axis_size(axis)
    pairs = [(source, (source + steps) % count) for source in range(count)]
    return lax.ppermute(value, axis, pairs)


def unit_rows(values):
    wide = values.astype(jnp.float32)
    return (wide * lax.rsqrt(jnp.sum(wide * wide, axis=-1, keepdims=True) + 1e-06)).astype(
        jnp.bfloat16
    )


def pick_row(table, index):
    hits = (jnp.arange(table.shape[0], dtype=jnp.int32) == index).astype(table.dtype)
    return jnp.sum(table * hits[:, None], axis=0)


def on_device(embeddings, cluster_ids, owners, pattern):
    n_own = lax.axis_size("own")
    n_grp = lax.axis_size("grp")
    tiles_here, tile_rows, width = embeddings.shape
    slots = n_own * CAPACITY
    units = unit_rows(embeddings)
    target_owner = owners[:, 0]
    hits = (target_owner[:, None] == jnp.arange(n_own, dtype=jnp.int32)[None, :]).astype(jnp.int32)
    before = jnp.cumsum(hits, axis=0) - hits
    slot = jnp.sum(before * hits, axis=1)
    position = target_owner * CAPACITY + slot
    placed = (position[:, None] == jnp.arange(slots, dtype=jnp.int32)[None, :]).astype(jnp.int32)
    filled = jnp.sum(placed, axis=0) > 0
    source = jnp.sum(placed * jnp.arange(tiles_here, dtype=jnp.int32)[:, None], axis=0)
    send_units = jnp.where(filled[:, None, None], units[source], jnp.zeros((), jnp.bfloat16))
    send_ids = jnp.where(filled[:, None], cluster_ids[source], -1)
    send_units = send_units.reshape(n_own, CAPACITY, tile_rows, width)
    send_ids = send_ids.reshape(n_own, CAPACITY, tile_rows)
    got_units, got_ids = (
        lax.all_to_all(send_units, "own", split_axis=0, concat_axis=0, tiled=True),
        lax.all_to_all(send_ids, "own", split_axis=0, concat_axis=0, tiled=True),
    )
    panel_rows = slots * tile_rows
    panel_units = got_units.reshape(panel_rows, width)
    panel_ids = got_ids.reshape(panel_rows)
    group = lax.axis_index("grp")
    allowed_row = pick_row(pattern, group)
    query_index = group * panel_rows + jnp.arange(panel_rows, dtype=jnp.int32)
    group_numbers = jnp.arange(n_grp, dtype=jnp.int32)

    def compare(best, piece, start):
        key_units, key_ids = piece
        count = key_ids.shape[0]
        key_index = start + jnp.arange(count, dtype=jnp.int32)
        key_group = key_index // panel_rows
        group_hits = (key_group[:, None] == group_numbers[None, :]).astype(jnp.int32)
        allowed = jnp.sum(group_hits * allowed_row[None, :], axis=1) > 0
        scores = lax.dot_general(
            panel_units, key_units, (((1,), (1,)), ((), ())), preferred_element_type=jnp.float32
        )
        match = (panel_ids[:, None] == key_ids[None, :]) & (panel_ids[:, None] >= 0)
        match = match & allowed[None, :] & (query_index[:, None] != key_index[None, :])
        return jnp.maximum(best, jnp.max(jnp.where(match, scores, jnp.float32(-1.0)), axis=1))

    start_best = jnp.full((panel_rows,), -1.0, dtype=jnp.float32)
    own_best = compare(start_best, (panel_units, panel_ids), group * panel_rows)

    def cycle_step(step, carry):
        current, moving_units, moving_ids = carry
        moving_units, moving_ids = passed_along((moving_units, moving_ids), "grp", 1)
        anchor = (group - step) % n_grp
        current = compare(current, (moving_units, moving_ids), anchor * panel_rows)
        return (current, moving_units, moving_ids)

    best = lax.fori_loop(1, n_grp, cycle_step, (own_best, panel_units, panel_ids))[0]
    returned = lax.all_to_all(
        best.reshape(n_own, CAPACITY, tile_rows), "own", split_axis=0, concat_axis=0, tiled=True
    )
    flat_best = returned.reshape(slots, tile_rows)
    return flat_best[position]


def solution(mesh):
    placed = (P(("grp", "own"), None, None), P(("grp", "own"), None), P(("grp", "own"), None), P())
    return jax.shard_map(
        on_device, mesh=mesh, in_specs=placed, out_specs=P(("grp", "own"), None), check_vma=False
    )
```

profile of v0, /device:TPU:32, one launch (start us, length us, event | category | flops | bytes accessed | tf_op | source)
XLA Modules:
  0.0 639.3 jit_solution(15200949319345338645)
XLA Ops:
  2.4 8.6 %all-to-all-start = ((s32[8,2,32]{2,1,0:T(2,128)}), s32[8,2,32]{2,1,0:T(2,128)S(1)}, u32[]{:S(2)}, u32[]{:S(2)}) async-start(s32[8,2,32]{2,1,0:T(2,128)} %broadcast_select_fusion.1), calls=%async_computation | async-start | bytes 16384 | tf_op jit(solution)/shard_map/all_to_all | solution.py:47
  11.0 1.2 fusion.8
  13.0 1.1 broadcast_select_fusion
  14.1 3.1 all-to-all-done
  17.3 4.9 all-to-all-start.1
  23.3 25.0 %all-to-all-done.1 = bf16[8,2,32,1024]{3,2,1,0:T(8,128)(2,1)S(1)} async-done(((bf16[8,2,32,1024]{3,2,1,0:T(8,128)(2,1)}), bf16[8,2,32,1024]{3,2,1,0:T(8,128)(2,1)S(1)}, u32[]{:S(2)}, u32[]{:S(2)}) %all-to-all-start.1) | async-done | bytes 1048608 | tf_op jit(solution)/shard_map/all_to_all | solution.py:46
  48.4 0.9 fusion.7
  49.2 577.2 %while.21 = (s32[]{:T(128)}, f32[512]{0:T(512)S(1)}, bf16[512,1024]{1,0:T(8,128)(2,1)S(1)}, s32[512]{0:T(512)S(1)}, s32[8,2,32]{2,1,0:T(2,128)}, /*index=5*/s32[...) while((s32[]{:T(128)}, f32[512]{0:T(512)S(1)}, ...), condition=%wide.wide.region_11.12_spmd.clone, body=%wide.wide.region_8.11_spmd.clone.sunk | while | flops 538764800 | bytes 8434158 | solution.py:81
  49.3 1.6 collective-permute-start
  51.1 15.8 %collective-permute-done = s32[512]{0:T(512)S(1)} collective-permute-done((s32[512]{0:T(512)S(1)}, s32[512]{0:T(512)S(1)}, u32[]{:S(2)}, u32[]{:S(2)}) %collective-permute-start) | collective-permute-done | bytes 2080 | tf_op jit(solution)/shard_map/while/body/eval_jaxpr/ppermute | solution.py:12
  66.9 0.9 select_reduce_fusion.10
  68.2 17.3 %collective-permute-done = s32[512]{0:T(512)S(1)} collective-permute-done((s32[512]{0:T(512)S(1)}, s32[512]{0:T(512)S(1)}, u32[]{:S(2)}, u32[]{:S(2)}) %collective-permute-start) | collective-permute-done | bytes 2080 | tf_op jit(solution)/shard_map/while/body/eval_jaxpr/ppermute | solution.py:12
  86.8 17.3 %collective-permute-done = s32[512]{0:T(512)S(1)} collective-permute-done((s32[512]{0:T(512)S(1)}, s32[512]{0:T(512)S(1)}, u32[]{:S(2)}, u32[]{:S(2)}) %collective-permute-start) | collective-permute-done | bytes 2080 | tf_op jit(solution)/shard_map/while/body/eval_jaxpr/ppermute | solution.py:12
  104.2 0.9 select_reduce_fusion.10
  105.5 17.3 %collective-permute-done = s32[512]{0:T(512)S(1)} collective-permute-done((s32[512]{0:T(512)S(1)}, s32[512]{0:T(512)S(1)}, u32[]{:S(2)}, u32[]{:S(2)}) %collective-permute-start) | collective-permute-done | bytes 2080 | tf_op jit(solution)/shard_map/while/body/eval_jaxpr/ppermute | solution.py:12
  124.1 17.3 %collective-permute-done = s32[512]{0:T(512)S(1)} collective-permute-done((s32[512]{0:T(512)S(1)}, s32[512]{0:T(512)S(1)}, u32[]{:S(2)}, u32[]{:S(2)}) %collective-permute-start) | collective-permute-done | bytes 2080 | tf_op jit(solution)/shard_map/while/body/eval_jaxpr/ppermute | solution.py:12
  142.7 17.3 %collective-permute-done = s32[512]{0:T(512)S(1)} collective-permute-done((s32[512]{0:T(512)S(1)}, s32[512]{0:T(512)S(1)}, u32[]{:S(2)}, u32[]{:S(2)}) %collective-permute-start) | collective-permute-done | bytes 2080 | tf_op jit(solution)/shard_map/while/body/eval_jaxpr/ppermute | solution.py:12
  161.3 17.3 %collective-permute-done = s32[512]{0:T(512)S(1)} collective-permute-done((s32[512]{0:T(512)S(1)}, s32[512]{0:T(512)S(1)}, u32[]{:S(2)}, u32[]{:S(2)}) %collective-permute-start) | collective-permute-done | bytes 2080 | tf_op jit(solution)/shard_map/while/body/eval_jaxpr/ppermute | solution.py:12
  179.9 17.3 %collective-permute-done = s32[512]{0:T(512)S(1)} collective-permute-done((s32[512]{0:T(512)S(1)}, s32[512]{0:T(512)S(1)}, u32[]{:S(2)}, u32[]{:S(2)}) %collective-permute-start) | collective-permute-done | bytes 2080 | tf_op jit(solution)/shard_map/while/body/eval_jaxpr/ppermute | solution.py:12
  198.6 17.3 %collective-permute-done = s32[512]{0:T(512)S(1)} collective-permute-done((s32[512]{0:T(512)S(1)}, s32[512]{0:T(512)S(1)}, u32[]{:S(2)}, u32[]{:S(2)}) %collective-permute-start) | collective-permute-done | bytes 2080 | tf_op jit(solution)/shard_map/while/body/eval_jaxpr/ppermute | solution.py:12
  217.2 17.3 %collective-permute-done = s32[512]{0:T(512)S(1)} collective-permute-done((s32[512]{0:T(512)S(1)}, s32[512]{0:T(512)S(1)}, u32[]{:S(2)}, u32[]{:S(2)}) %collective-permute-start) | collective-permute-done | bytes 2080 | tf_op jit(solution)/shard_map/while/body/eval_jaxpr/ppermute | solution.py:12
  235.8 17.3 %collective-permute-done = s32[512]{0:T(512)S(1)} collective-permute-done((s32[512]{0:T(512)S(1)}, s32[512]{0:T(512)S(1)}, u32[]{:S(2)}, u32[]{:S(2)}) %collective-permute-start) | collective-permute-done | bytes 2080 | tf_op jit(solution)/shard_map/while/body/eval_jaxpr/ppermute | solution.py:12
  254.4 17.3 %collective-permute-done = s32[512]{0:T(512)S(1)} collective-permute-done((s32[512]{0:T(512)S(1)}, s32[512]{0:T(512)S(1)}, u32[]{:S(2)}, u32[]{:S(2)}) %collective-permute-start) | collective-permute-done | bytes 2080 | tf_op jit(solution)/shard_map/while/body/eval_jaxpr/ppermute | solution.py:12
  273.0 17.3 %collective-permute-done = s32[512]{0:T(512)S(1)} collective-permute-done((s32[512]{0:T(512)S(1)}, s32[512]{0:T(512)S(1)}, u32[]{:S(2)}, u32[]{:S(2)}) %collective-permute-start) | collective-permute-done | bytes 2080 | tf_op jit(solution)/shard_map/while/body/eval_jaxpr/ppermute | solution.py:12
  291.7 17.3 %collective-permute-done = s32[512]{0:T(512)S(1)} collective-permute-done((s32[512]{0:T(512)S(1)}, s32[512]{0:T(512)S(1)}, u32[]{:S(2)}, u32[]{:S(2)}) %collective-permute-start) | collective-permute-done | bytes 2080 | tf_op jit(solution)/shard_map/while/body/eval_jaxpr/ppermute | solution.py:12
  310.3 17.3 %collective-permute-done = s32[512]{0:T(512)S(1)} collective-permute-done((s32[512]{0:T(512)S(1)}, s32[512]{0:T(512)S(1)}, u32[]{:S(2)}, u32[]{:S(2)}) %collective-permute-start) | collective-permute-done | bytes 2080 | tf_op jit(solution)/shard_map/while/body/eval_jaxpr/ppermute | solution.py:12
  328.9 17.3 %collective-permute-done = s32[512]{0:T(512)S(1)} collective-permute-done((s32[512]{0:T(512)S(1)}, s32[512]{0:T(512)S(1)}, u32[]{:S(2)}, u32[]{:S(2)}) %collective-permute-start) | collective-permute-done | bytes 2080 | tf_op jit(solution)/shard_map/while/body/eval_jaxpr/ppermute | solution.py:12
  346.2 0.9 select_reduce_fusion.10
  347.5 17.3 %collective-permute-done = s32[512]{0:T(512)S(1)} collective-permute-done((s32[512]{0:T(512)S(1)}, s32[512]{0:T(512)S(1)}, u32[]{:S(2)}, u32[]{:S(2)}) %collective-permute-start) | collective-permute-done | bytes 2080 | tf_op jit(solution)/shard_map/while/body/eval_jaxpr/ppermute | solution.py:12
  366.2 17.3 %collective-permute-done = s32[512]{0:T(512)S(1)} collective-permute-done((s32[512]{0:T(512)S(1)}, s32[512]{0:T(512)S(1)}, u32[]{:S(2)}, u32[]{:S(2)}) %collective-permute-start) | collective-permute-done | bytes 2080 | tf_op jit(solution)/shard_map/while/body/eval_jaxpr/ppermute | solution.py:12
  384.8 17.3 %collective-permute-done = s32[512]{0:T(512)S(1)} collective-permute-done((s32[512]{0:T(512)S(1)}, s32[512]{0:T(512)S(1)}, u32[]{:S(2)}, u32[]{:S(2)}) %collective-permute-start) | collective-permute-done | bytes 2080 | tf_op jit(solution)/shard_map/while/body/eval_jaxpr/ppermute | solution.py:12
  403.4 17.3 %collective-permute-done = s32[512]{0:T(512)S(1)} collective-permute-done((s32[512]{0:T(512)S(1)}, s32[512]{0:T(512)S(1)}, u32[]{:S(2)}, u32[]{:S(2)}) %collective-permute-start) | collective-permute-done | bytes 2080 | tf_op jit(solution)/shard_map/while/body/eval_jaxpr/ppermute | solution.py:12
  422.0 17.3 %collective-permute-done = s32[512]{0:T(512)S(1)} collective-permute-done((s32[512]{0:T(512)S(1)}, s32[512]{0:T(512)S(1)}, u32[]{:S(2)}, u32[]{:S(2)}) %collective-permute-start) | collective-permute-done | bytes 2080 | tf_op jit(solution)/shard_map/while/body/eval_jaxpr/ppermute | solution.py:12
  439.3 0.9 select_reduce_fusion.10
  440.6 17.3 %collective-permute-done = s32[512]{0:T(512)S(1)} collective-permute-done((s32[512]{0:T(512)S(1)}, s32[512]{0:T(512)S(1)}, u32[]{:S(2)}, u32[]{:S(2)}) %collective-permute-start) | collective-permute-done | bytes 2080 | tf_op jit(solution)/shard_map/while/body/eval_jaxpr/ppermute | solution.py:12
  459.3 17.3 %collective-permute-done = s32[512]{0:T(512)S(1)} collective-permute-done((s32[512]{0:T(512)S(1)}, s32[512]{0:T(512)S(1)}, u32[]{:S(2)}, u32[]{:S(2)}) %collective-permute-start) | collective-permute-done | bytes 2080 | tf_op jit(solution)/shard_map/while/body/eval_jaxpr/ppermute | solution.py:12
  477.9 17.3 %collective-permute-done = s32[512]{0:T(512)S(1)} collective-permute-done((s32[512]{0:T(512)S(1)}, s32[512]{0:T(512)S(1)}, u32[]{:S(2)}, u32[]{:S(2)}) %collective-permute-start) | collective-permute-done | bytes 2080 | tf_op jit(solution)/shard_map/while/body/eval_jaxpr/ppermute | solution.py:12
  496.5 17.3 %collective-permute-done = s32[512]{0:T(512)S(1)} collective-permute-done((s32[512]{0:T(512)S(1)}, s32[512]{0:T(512)S(1)}, u32[]{:S(2)}, u32[]{:S(2)}) %collective-permute-start) | collective-permute-done | bytes 2080 | tf_op jit(solution)/shard_map/while/body/eval_jaxpr/ppermute | solution.py:12
  515.1 17.3 %collective-permute-done = s32[512]{0:T(512)S(1)} collective-permute-done((s32[512]{0:T(512)S(1)}, s32[512]{0:T(512)S(1)}, u32[]{:S(2)}, u32[]{:S(2)}) %collective-permute-start) | collective-permute-done | bytes 2080 | tf_op jit(solution)/shard_map/while/body/eval_jaxpr/ppermute | solution.py:12
  532.4 0.9 select_reduce_fusion.10
  533.7 17.3 %collective-permute-done = s32[512]{0:T(512)S(1)} collective-permute-done((s32[512]{0:T(512)S(1)}, s32[512]{0:T(512)S(1)}, u32[]{:S(2)}, u32[]{:S(2)}) %collective-permute-start) | collective-permute-done | bytes 2080 | tf_op jit(solution)/shard_map/while/body/eval_jaxpr/ppermute | solution.py:12
  552.4 17.3 %collective-permute-done = s32[512]{0:T(512)S(1)} collective-permute-done((s32[512]{0:T(512)S(1)}, s32[512]{0:T(512)S(1)}, u32[]{:S(2)}, u32[]{:S(2)}) %collective-permute-start) | collective-permute-done | bytes 2080 | tf_op jit(solution)/shard_map/while/body/eval_jaxpr/ppermute | solution.py:12
  571.0 17.3 %collective-permute-done = s32[512]{0:T(512)S(1)} collective-permute-done((s32[512]{0:T(512)S(1)}, s32[512]{0:T(512)S(1)}, u32[]{:S(2)}, u32[]{:S(2)}) %collective-permute-start) | collective-permute-done | bytes 2080 | tf_op jit(solution)/shard_map/while/body/eval_jaxpr/ppermute | solution.py:12
  589.6 17.3 %collective-permute-done = s32[512]{0:T(512)S(1)} collective-permute-done((s32[512]{0:T(512)S(1)}, s32[512]{0:T(512)S(1)}, u32[]{:S(2)}, u32[]{:S(2)}) %collective-permute-start) | collective-permute-done | bytes 2080 | tf_op jit(solution)/shard_map/while/body/eval_jaxpr/ppermute | solution.py:12
  608.2 17.3 %collective-permute-done = s32[512]{0:T(512)S(1)} collective-permute-done((s32[512]{0:T(512)S(1)}, s32[512]{0:T(512)S(1)}, u32[]{:S(2)}, u32[]{:S(2)}) %collective-permute-start) | collective-permute-done | bytes 2080 | tf_op jit(solution)/shard_map/while/body/eval_jaxpr/ppermute | solution.py:12
  627.2 4.7 all-to-all-start.2
  631.9 6.3 all-to-all-done.2
  638.2 1.1 gather_fusion.2
  (372 shorter events, 38.8 us)
Async XLA Ops:
  17.3 31.0 %all-to-all-start.1 = ((bf16[8,2,32,1024]{3,2,1,0:T(8,128)(2,1)}), bf16[8,2,32,1024]{3,2,1,0:T(8,128)(2,1)S(1)}, u32[]{:S(2)}, u32[]{:S(2)}) async-start(bf16[8,2,32,1024]{3,2,1,0:T(8,128)(2,1)} %broadcast_select_fusion), calls=%async_computation.1 | async-start | bytes 2097152 | tf_op jit(solution)/shard_map/all_to_all | solution.py:46
  49.3 17.6 %collective-permute-start.1 = (bf16[512,1024]{1,0:T(8,128)(2,1)S(1)}, bf16[512,1024]{1,0:T(8,128)(2,1)S(1)}, u32[]{:S(2)}, u32[]{:S(2)}) collective-permute-start(bf16[512,1024]{1,0:T(8,128)(2,1)S(1)} %get-tuple-element.425), channel_id=1, source_target_pairs={{0,8},{8,16},{16,24},{24,32},{32,40},{40,48},{48,56},{56,64},{64,7... | collective-permute-start | bytes 3145736 | tf_op jit(solution)/shard_map/while/body/eval_jaxpr/ppermute | solution.py:12
  49.3 17.6 %collective-permute-start = (s32[512]{0:T(512)S(1)}, s32[512]{0:T(512)S(1)}, u32[]{:S(2)}, u32[]{:S(2)}) collective-permute-start(s32[512]{0:T(512)S(1)} %get-tuple-element.426), channel_id=1, source_target_pairs={{0,8},{8,16},{16,24},{24,32},{32,40},{40,48},{48,56},{56,64},{64,7... | collective-permute-start | bytes 6152 | tf_op jit(solution)/shard_map/while/body/eval_jaxpr/ppermute | solution.py:12
  67.9 17.6 %collective-permute-start.1 = (bf16[512,1024]{1,0:T(8,128)(2,1)S(1)}, bf16[512,1024]{1,0:T(8,128)(2,1)S(1)}, u32[]{:S(2)}, u32[]{:S(2)}) collective-permute-start(bf16[512,1024]{1,0:T(8,128)(2,1)S(1)} %get-tuple-element.425), channel_id=1, source_target_pairs={{0,8},{8,16},{16,24},{24,32},{32,40},{40,48},{48,56},{56,64},{64,7... | collective-permute-start | bytes 3145736 | tf_op jit(solution)/shard_map/while/body/eval_jaxpr/ppermute | solution.py:12
  68.0 17.6 %collective-permute-start = (s32[512]{0:T(512)S(1)}, s32[512]{0:T(512)S(1)}, u32[]{:S(2)}, u32[]{:S(2)}) collective-permute-start(s32[512]{0:T(512)S(1)} %get-tuple-element.426), channel_id=1, source_target_pairs={{0,8},{8,16},{16,24},{24,32},{32,40},{40,48},{48,56},{56,64},{64,7... | collective-permute-start | bytes 6152 | tf_op jit(solution)/shard_map/while/body/eval_jaxpr/ppermute | solution.py:12
  86.5 17.6 %collective-permute-start.1 = (bf16[512,1024]{1,0:T(8,128)(2,1)S(1)}, bf16[512,1024]{1,0:T(8,128)(2,1)S(1)}, u32[]{:S(2)}, u32[]{:S(2)}) collective-permute-start(bf16[512,1024]{1,0:T(8,128)(2,1)S(1)} %get-tuple-element.425), channel_id=1, source_target_pairs={{0,8},{8,16},{16,24},{24,32},{32,40},{40,48},{48,56},{56,64},{64,7... | collective-permute-start | bytes 3145736 | tf_op jit(solution)/shard_map/while/body/eval_jaxpr/ppermute | solution.py:12
  86.6 17.6 %collective-permute-start = (s32[512]{0:T(512)S(1)}, s32[512]{0:T(512)S(1)}, u32[]{:S(2)}, u32[]{:S(2)}) collective-permute-start(s32[512]{0:T(512)S(1)} %get-tuple-element.426), channel_id=1, source_target_pairs={{0,8},{8,16},{16,24},{24,32},{32,40},{40,48},{48,56},{56,64},{64,7... | collective-permute-start | bytes 6152 | tf_op jit(solution)/shard_map/while/body/eval_jaxpr/ppermute | solution.py:12
  105.1 17.6 %collective-permute-start.1 = (bf16[512,1024]{1,0:T(8,128)(2,1)S(1)}, bf16[512,1024]{1,0:T(8,128)(2,1)S(1)}, u32[]{:S(2)}, u32[]{:S(2)}) collective-permute-start(bf16[512,1024]{1,0:T(8,128)(2,1)S(1)} %get-tuple-element.425), channel_id=1, source_target_pairs={{0,8},{8,16},{16,24},{24,32},{32,40},{40,48},{48,56},{56,64},{64,7... | collective-permute-start | bytes 3145736 | tf_op jit(solution)/shard_map/while/body/eval_jaxpr/ppermute | solution.py:12
  105.2 17.6 %collective-permute-start = (s32[512]{0:T(512)S(1)}, s32[512]{0:T(512)S(1)}, u32[]{:S(2)}, u32[]{:S(2)}) collective-permute-start(s32[512]{0:T(512)S(1)} %get-tuple-element.426), channel_id=1, source_target_pairs={{0,8},{8,16},{16,24},{24,32},{32,40},{40,48},{48,56},{56,64},{64,7... | collective-permute-start | bytes 6152 | tf_op jit(solution)/shard_map/while/body/eval_jaxpr/ppermute | solution.py:12
  123.7 17.6 %collective-permute-start.1 = (bf16[512,1024]{1,0:T(8,128)(2,1)S(1)}, bf16[512,1024]{1,0:T(8,128)(2,1)S(1)}, u32[]{:S(2)}, u32[]{:S(2)}) collective-permute-start(bf16[512,1024]{1,0:T(8,128)(2,1)S(1)} %get-tuple-element.425), channel_id=1, source_target_pairs={{0,8},{8,16},{16,24},{24,32},{32,40},{40,48},{48,56},{56,64},{64,7... | collective-permute-start | bytes 3145736 | tf_op jit(solution)/shard_map/while/body/eval_jaxpr/ppermute | solution.py:12
  123.8 17.6 %collective-permute-start = (s32[512]{0:T(512)S(1)}, s32[512]{0:T(512)S(1)}, u32[]{:S(2)}, u32[]{:S(2)}) collective-permute-start(s32[512]{0:T(512)S(1)} %get-tuple-element.426), channel_id=1, source_target_pairs={{0,8},{8,16},{16,24},{24,32},{32,40},{40,48},{48,56},{56,64},{64,7... | collective-permute-start | bytes 6152 | tf_op jit(solution)/shard_map/while/body/eval_jaxpr/ppermute | solution.py:12
  142.4 17.6 %collective-permute-start.1 = (bf16[512,1024]{1,0:T(8,128)(2,1)S(1)}, bf16[512,1024]{1,0:T(8,128)(2,1)S(1)}, u32[]{:S(2)}, u32[]{:S(2)}) collective-permute-start(bf16[512,1024]{1,0:T(8,128)(2,1)S(1)} %get-tuple-element.425), channel_id=1, source_target_pairs={{0,8},{8,16},{16,24},{24,32},{32,40},{40,48},{48,56},{56,64},{64,7... | collective-permute-start | bytes 3145736 | tf_op jit(solution)/shard_map/while/body/eval_jaxpr/ppermute | solution.py:12
  142.5 17.6 %collective-permute-start = (s32[512]{0:T(512)S(1)}, s32[512]{0:T(512)S(1)}, u32[]{:S(2)}, u32[]{:S(2)}) collective-permute-start(s32[512]{0:T(512)S(1)} %get-tuple-element.426), channel_id=1, source_target_pairs={{0,8},{8,16},{16,24},{24,32},{32,40},{40,48},{48,56},{56,64},{64,7... | collective-permute-start | bytes 6152 | tf_op jit(solution)/shard_map/while/body/eval_jaxpr/ppermute | solution.py:12
  161.0 17.6 %collective-permute-start.1 = (bf16[512,1024]{1,0:T(8,128)(2,1)S(1)}, bf16[512,1024]{1,0:T(8,128)(2,1)S(1)}, u32[]{:S(2)}, u32[]{:S(2)}) collective-permute-start(bf16[512,1024]{1,0:T(8,128)(2,1)S(1)} %get-tuple-element.425), channel_id=1, source_target_pairs={{0,8},{8,16},{16,24},{24,32},{32,40},{40,48},{48,56},{56,64},{64,7... | collective-permute-start | bytes 3145736 | tf_op jit(solution)/shard_map/while/body/eval_jaxpr/ppermute | solution.py:12
  161.1 17.6 %collective-permute-start = (s32[512]{0:T(512)S(1)}, s32[512]{0:T(512)S(1)}, u32[]{:S(2)}, u32[]{:S(2)}) collective-permute-start(s32[512]{0:T(512)S(1)} %get-tuple-element.426), channel_id=1, source_target_pairs={{0,8},{8,16},{16,24},{24,32},{32,40},{40,48},{48,56},{56,64},{64,7... | collective-permute-start | bytes 6152 | tf_op jit(solution)/shard_map/while/body/eval_jaxpr/ppermute | solution.py:12
  179.6 17.6 %collective-permute-start.1 = (bf16[512,1024]{1,0:T(8,128)(2,1)S(1)}, bf16[512,1024]{1,0:T(8,128)(2,1)S(1)}, u32[]{:S(2)}, u32[]{:S(2)}) collective-permute-start(bf16[512,1024]{1,0:T(8,128)(2,1)S(1)} %get-tuple-element.425), channel_id=1, source_target_pairs={{0,8},{8,16},{16,24},{24,32},{32,40},{40,48},{48,56},{56,64},{64,7... | collective-permute-start | bytes 3145736 | tf_op jit(solution)/shard_map/while/body/eval_jaxpr/ppermute | solution.py:12
  179.7 17.6 %collective-permute-start = (s32[512]{0:T(512)S(1)}, s32[512]{0:T(512)S(1)}, u32[]{:S(2)}, u32[]{:S(2)}) collective-permute-start(s32[512]{0:T(512)S(1)} %get-tuple-element.426), channel_id=1, source_target_pairs={{0,8},{8,16},{16,24},{24,32},{32,40},{40,48},{48,56},{56,64},{64,7... | collective-permute-start | bytes 6152 | tf_op jit(solution)/shard_map/while/body/eval_jaxpr/ppermute | solution.py:12
  198.2 17.6 %collective-permute-start.1 = (bf16[512,1024]{1,0:T(8,128)(2,1)S(1)}, bf16[512,1024]{1,0:T(8,128)(2,1)S(1)}, u32[]{:S(2)}, u32[]{:S(2)}) collective-permute-start(bf16[512,1024]{1,0:T(8,128)(2,1)S(1)} %get-tuple-element.425), channel_id=1, source_target_pairs={{0,8},{8,16},{16,24},{24,32},{32,40},{40,48},{48,56},{56,64},{64,7... | collective-permute-start | bytes 3145736 | tf_op jit(solution)/shard_map/while/body/eval_jaxpr/ppermute | solution.py:12
  198.3 17.6 %collective-permute-start = (s32[512]{0:T(512)S(1)}, s32[512]{0:T(512)S(1)}, u32[]{:S(2)}, u32[]{:S(2)}) collective-permute-start(s32[512]{0:T(512)S(1)} %get-tuple-element.426), channel_id=1, source_target_pairs={{0,8},{8,16},{16,24},{24,32},{32,40},{40,48},{48,56},{56,64},{64,7... | collective-permute-start | bytes 6152 | tf_op jit(solution)/shard_map/while/body/eval_jaxpr/ppermute | solution.py:12
  216.9 17.6 %collective-permute-start.1 = (bf16[512,1024]{1,0:T(8,128)(2,1)S(1)}, bf16[512,1024]{1,0:T(8,128)(2,1)S(1)}, u32[]{:S(2)}, u32[]{:S(2)}) collective-permute-start(bf16[512,1024]{1,0:T(8,128)(2,1)S(1)} %get-tuple-element.425), channel_id=1, source_target_pairs={{0,8},{8,16},{16,24},{24,32},{32,40},{40,48},{48,56},{56,64},{64,7... | collective-permute-start | bytes 3145736 | tf_op jit(solution)/shard_map/while/body/eval_jaxpr/ppermute | solution.py:12
  235.5 17.6 %collective-permute-start.1 = (bf16[512,1024]{1,0:T(8,128)(2,1)S(1)}, bf16[512,1024]{1,0:T(8,128)(2,1)S(1)}, u32[]{:S(2)}, u32[]{:S(2)}) collective-permute-start(bf16[512,1024]{1,0:T(8,128)(2,1)S(1)} %get-tuple-element.425), channel_id=1, source_target_pairs={{0,8},{8,16},{16,24},{24,32},{32,40},{40,48},{48,56},{56,64},{64,7... | collective-permute-start | bytes 3145736 | tf_op jit(solution)/shard_map/while/body/eval_jaxpr/ppermute | solution.py:12
  254.1 17.6 %collective-permute-start.1 = (bf16[512,1024]{1,0:T(8,128)(2,1)S(1)}, bf16[512,1024]{1,0:T(8,128)(2,1)S(1)}, u32[]{:S(2)}, u32[]{:S(2)}) collective-permute-start(bf16[512,1024]{1,0:T(8,128)(2,1)S(1)} %get-tuple-element.425), channel_id=1, source_target_pairs={{0,8},{8,16},{16,24},{24,32},{32,40},{40,48},{48,56},{56,64},{64,7... | collective-permute-start | bytes 3145736 | tf_op jit(solution)/shard_map/while/body/eval_jaxpr/ppermute | solution.py:12
  254.2 17.6 %collective-permute-start = (s32[512]{0:T(512)S(1)}, s32[512]{0:T(512)S(1)}, u32[]{:S(2)}, u32[]{:S(2)}) collective-permute-start(s32[512]{0:T(512)S(1)} %get-tuple-element.426), channel_id=1, source_target_pairs={{0,8},{8,16},{16,24},{24,32},{32,40},{40,48},{48,56},{56,64},{64,7... | collective-permute-start | bytes 6152 | tf_op jit(solution)/shard_map/while/body/eval_jaxpr/ppermute | solution.py:12
  272.7 17.6 %collective-permute-start.1 = (bf16[512,1024]{1,0:T(8,128)(2,1)S(1)}, bf16[512,1024]{1,0:T(8,128)(2,1)S(1)}, u32[]{:S(2)}, u32[]{:S(2)}) collective-permute-start(bf16[512,1024]{1,0:T(8,128)(2,1)S(1)} %get-tuple-element.425), channel_id=1, source_target_pairs={{0,8},{8,16},{16,24},{24,32},{32,40},{40,48},{48,56},{56,64},{64,7... | collective-permute-start | bytes 3145736 | tf_op jit(solution)/shard_map/while/body/eval_jaxpr/ppermute | solution.py:12
  291.3 17.6 %collective-permute-start.1 = (bf16[512,1024]{1,0:T(8,128)(2,1)S(1)}, bf16[512,1024]{1,0:T(8,128)(2,1)S(1)}, u32[]{:S(2)}, u32[]{:S(2)}) collective-permute-start(bf16[512,1024]{1,0:T(8,128)(2,1)S(1)} %get-tuple-element.425), channel_id=1, source_target_pairs={{0,8},{8,16},{16,24},{24,32},{32,40},{40,48},{48,56},{56,64},{64,7... | collective-permute-start | bytes 3145736 | tf_op jit(solution)/shard_map/while/body/eval_jaxpr/ppermute | solution.py:12
  310.0 17.6 %collective-permute-start.1 = (bf16[512,1024]{1,0:T(8,128)(2,1)S(1)}, bf16[512,1024]{1,0:T(8,128)(2,1)S(1)}, u32[]{:S(2)}, u32[]{:S(2)}) collective-permute-start(bf16[512,1024]{1,0:T(8,128)(2,1)S(1)} %get-tuple-element.425), channel_id=1, source_target_pairs={{0,8},{8,16},{16,24},{24,32},{32,40},{40,48},{48,56},{56,64},{64,7... | collective-permute-start | bytes 3145736 | tf_op jit(solution)/shard_map/while/body/eval_jaxpr/ppermute | solution.py:12
  310.0 17.6 %collective-permute-start = (s32[512]{0:T(512)S(1)}, s32[512]{0:T(512)S(1)}, u32[]{:S(2)}, u32[]{:S(2)}) collective-permute-start(s32[512]{0:T(512)S(1)} %get-tuple-element.426), channel_id=1, source_target_pairs={{0,8},{8,16},{16,24},{24,32},{32,40},{40,48},{48,56},{56,64},{64,7... | collective-permute-start | bytes 6152 | tf_op jit(solution)/shard_map/while/body/eval_jaxpr/ppermute | solution.py:12
  328.6 17.6 %collective-permute-start.1 = (bf16[512,1024]{1,0:T(8,128)(2,1)S(1)}, bf16[512,1024]{1,0:T(8,128)(2,1)S(1)}, u32[]{:S(2)}, u32[]{:S(2)}) collective-permute-start(bf16[512,1024]{1,0:T(8,128)(2,1)S(1)} %get-tuple-element.425), channel_id=1, source_target_pairs={{0,8},{8,16},{16,24},{24,32},{32,40},{40,48},{48,56},{56,64},{64,7... | collective-permute-start | bytes 3145736 | tf_op jit(solution)/shard_map/while/body/eval_jaxpr/ppermute | solution.py:12
  347.2 17.6 %collective-permute-start.1 = (bf16[512,1024]{1,0:T(8,128)(2,1)S(1)}, bf16[512,1024]{1,0:T(8,128)(2,1)S(1)}, u32[]{:S(2)}, u32[]{:S(2)}) collective-permute-start(bf16[512,1024]{1,0:T(8,128)(2,1)S(1)} %get-tuple-element.425), channel_id=1, source_target_pairs={{0,8},{8,16},{16,24},{24,32},{32,40},{40,48},{48,56},{56,64},{64,7... | collective-permute-start | bytes 3145736 | tf_op jit(solution)/shard_map/while/body/eval_jaxpr/ppermute | solution.py:12
  347.3 17.6 %collective-permute-start = (s32[512]{0:T(512)S(1)}, s32[512]{0:T(512)S(1)}, u32[]{:S(2)}, u32[]{:S(2)}) collective-permute-start(s32[512]{0:T(512)S(1)} %get-tuple-element.426), channel_id=1, source_target_pairs={{0,8},{8,16},{16,24},{24,32},{32,40},{40,48},{48,56},{56,64},{64,7... | collective-permute-start | bytes 6152 | tf_op jit(solution)/shard_map/while/body/eval_jaxpr/ppermute | solution.py:12
  365.8 17.6 %collective-permute-start.1 = (bf16[512,1024]{1,0:T(8,128)(2,1)S(1)}, bf16[512,1024]{1,0:T(8,128)(2,1)S(1)}, u32[]{:S(2)}, u32[]{:S(2)}) collective-permute-start(bf16[512,1024]{1,0:T(8,128)(2,1)S(1)} %get-tuple-element.425), channel_id=1, source_target_pairs={{0,8},{8,16},{16,24},{24,32},{32,40},{40,48},{48,56},{56,64},{64,7... | collective-permute-start | bytes 3145736 | tf_op jit(solution)/shard_map/while/body/eval_jaxpr/ppermute | solution.py:12
  384.4 17.6 %collective-permute-start.1 = (bf16[512,1024]{1,0:T(8,128)(2,1)S(1)}, bf16[512,1024]{1,0:T(8,128)(2,1)S(1)}, u32[]{:S(2)}, u32[]{:S(2)}) collective-permute-start(bf16[512,1024]{1,0:T(8,128)(2,1)S(1)} %get-tuple-element.425), channel_id=1, source_target_pairs={{0,8},{8,16},{16,24},{24,32},{32,40},{40,48},{48,56},{56,64},{64,7... | collective-permute-start | bytes 3145736 | tf_op jit(solution)/shard_map/while/body/eval_jaxpr/ppermute | solution.py:12
  403.1 17.6 %collective-permute-start.1 = (bf16[512,1024]{1,0:T(8,128)(2,1)S(1)}, bf16[512,1024]{1,0:T(8,128)(2,1)S(1)}, u32[]{:S(2)}, u32[]{:S(2)}) collective-permute-start(bf16[512,1024]{1,0:T(8,128)(2,1)S(1)} %get-tuple-element.425), channel_id=1, source_target_pairs={{0,8},{8,16},{16,24},{24,32},{32,40},{40,48},{48,56},{56,64},{64,7... | collective-permute-start | bytes 3145736 | tf_op jit(solution)/shard_map/while/body/eval_jaxpr/ppermute | solution.py:12
  403.1 17.6 %collective-permute-start = (s32[512]{0:T(512)S(1)}, s32[512]{0:T(512)S(1)}, u32[]{:S(2)}, u32[]{:S(2)}) collective-permute-start(s32[512]{0:T(512)S(1)} %get-tuple-element.426), channel_id=1, source_target_pairs={{0,8},{8,16},{16,24},{24,32},{32,40},{40,48},{48,56},{56,64},{64,7... | collective-permute-start | bytes 6152 | tf_op jit(solution)/shard_map/while/body/eval_jaxpr/ppermute | solution.py:12
  421.7 17.6 %collective-permute-start.1 = (bf16[512,1024]{1,0:T(8,128)(2,1)S(1)}, bf16[512,1024]{1,0:T(8,128)(2,1)S(1)}, u32[]{:S(2)}, u32[]{:S(2)}) collective-permute-start(bf16[512,1024]{1,0:T(8,128)(2,1)S(1)} %get-tuple-element.425), channel_id=1, source_target_pairs={{0,8},{8,16},{16,24},{24,32},{32,40},{40,48},{48,56},{56,64},{64,7... | collective-permute-start | bytes 3145736 | tf_op jit(solution)/shard_map/while/body/eval_jaxpr/ppermute | solution.py:12
  440.3 17.6 %collective-permute-start.1 = (bf16[512,1024]{1,0:T(8,128)(2,1)S(1)}, bf16[512,1024]{1,0:T(8,128)(2,1)S(1)}, u32[]{:S(2)}, u32[]{:S(2)}) collective-permute-start(bf16[512,1024]{1,0:T(8,128)(2,1)S(1)} %get-tuple-element.425), channel_id=1, source_target_pairs={{0,8},{8,16},{16,24},{24,32},{32,40},{40,48},{48,56},{56,64},{64,7... | collective-permute-start | bytes 3145736 | tf_op jit(solution)/shard_map/while/body/eval_jaxpr/ppermute | solution.py:12
  458.9 17.6 %collective-permute-start.1 = (bf16[512,1024]{1,0:T(8,128)(2,1)S(1)}, bf16[512,1024]{1,0:T(8,128)(2,1)S(1)}, u32[]{:S(2)}, u32[]{:S(2)}) collective-permute-start(bf16[512,1024]{1,0:T(8,128)(2,1)S(1)} %get-tuple-element.425), channel_id=1, source_target_pairs={{0,8},{8,16},{16,24},{24,32},{32,40},{40,48},{48,56},{56,64},{64,7... | collective-permute-start | bytes 3145736 | tf_op jit(solution)/shard_map/while/body/eval_jaxpr/ppermute | solution.py:12
  477.5 17.6 %collective-permute-start.1 = (bf16[512,1024]{1,0:T(8,128)(2,1)S(1)}, bf16[512,1024]{1,0:T(8,128)(2,1)S(1)}, u32[]{:S(2)}, u32[]{:S(2)}) collective-permute-start(bf16[512,1024]{1,0:T(8,128)(2,1)S(1)} %get-tuple-element.425), channel_id=1, source_target_pairs={{0,8},{8,16},{16,24},{24,32},{32,40},{40,48},{48,56},{56,64},{64,7... | collective-permute-start | bytes 3145736 | tf_op jit(solution)/shard_map/while/body/eval_jaxpr/ppermute | solution.py:12
  496.2 17.6 %collective-permute-start.1 = (bf16[512,1024]{1,0:T(8,128)(2,1)S(1)}, bf16[512,1024]{1,0:T(8,128)(2,1)S(1)}, u32[]{:S(2)}, u32[]{:S(2)}) collective-permute-start(bf16[512,1024]{1,0:T(8,128)(2,1)S(1)} %get-tuple-element.425), channel_id=1, source_target_pairs={{0,8},{8,16},{16,24},{24,32},{32,40},{40,48},{48,56},{56,64},{64,7... | collective-permute-start | bytes 3145736 | tf_op jit(solution)/shard_map/while/body/eval_jaxpr/ppermute | solution.py:12
  496.3 17.6 %collective-permute-start = (s32[512]{0:T(512)S(1)}, s32[512]{0:T(512)S(1)}, u32[]{:S(2)}, u32[]{:S(2)}) collective-permute-start(s32[512]{0:T(512)S(1)} %get-tuple-element.426), channel_id=1, source_target_pairs={{0,8},{8,16},{16,24},{24,32},{32,40},{40,48},{48,56},{56,64},{64,7... | collective-permute-start | bytes 6152 | tf_op jit(solution)/shard_map/while/body/eval_jaxpr/ppermute | solution.py:12
  514.8 17.6 %collective-permute-start.1 = (bf16[512,1024]{1,0:T(8,128)(2,1)S(1)}, bf16[512,1024]{1,0:T(8,128)(2,1)S(1)}, u32[]{:S(2)}, u32[]{:S(2)}) collective-permute-start(bf16[512,1024]{1,0:T(8,128)(2,1)S(1)} %get-tuple-element.425), channel_id=1, source_target_pairs={{0,8},{8,16},{16,24},{24,32},{32,40},{40,48},{48,56},{56,64},{64,7... | collective-permute-start | bytes 3145736 | tf_op jit(solution)/shard_map/while/body/eval_jaxpr/ppermute | solution.py:12
  533.4 17.6 %collective-permute-start.1 = (bf16[512,1024]{1,0:T(8,128)(2,1)S(1)}, bf16[512,1024]{1,0:T(8,128)(2,1)S(1)}, u32[]{:S(2)}, u32[]{:S(2)}) collective-permute-start(bf16[512,1024]{1,0:T(8,128)(2,1)S(1)} %get-tuple-element.425), channel_id=1, source_target_pairs={{0,8},{8,16},{16,24},{24,32},{32,40},{40,48},{48,56},{56,64},{64,7... | collective-permute-start | bytes 3145736 | tf_op jit(solution)/shard_map/while/body/eval_jaxpr/ppermute | solution.py:12
  552.0 17.6 %collective-permute-start.1 = (bf16[512,1024]{1,0:T(8,128)(2,1)S(1)}, bf16[512,1024]{1,0:T(8,128)(2,1)S(1)}, u32[]{:S(2)}, u32[]{:S(2)}) collective-permute-start(bf16[512,1024]{1,0:T(8,128)(2,1)S(1)} %get-tuple-element.425), channel_id=1, source_target_pairs={{0,8},{8,16},{16,24},{24,32},{32,40},{40,48},{48,56},{56,64},{64,7... | collective-permute-start | bytes 3145736 | tf_op jit(solution)/shard_map/while/body/eval_jaxpr/ppermute | solution.py:12
  570.6 17.6 %collective-permute-start.1 = (bf16[512,1024]{1,0:T(8,128)(2,1)S(1)}, bf16[512,1024]{1,0:T(8,128)(2,1)S(1)}, u32[]{:S(2)}, u32[]{:S(2)}) collective-permute-start(bf16[512,1024]{1,0:T(8,128)(2,1)S(1)} %get-tuple-element.425), channel_id=1, source_target_pairs={{0,8},{8,16},{16,24},{24,32},{32,40},{40,48},{48,56},{56,64},{64,7... | collective-permute-start | bytes 3145736 | tf_op jit(solution)/shard_map/while/body/eval_jaxpr/ppermute | solution.py:12
  570.7 17.6 %collective-permute-start = (s32[512]{0:T(512)S(1)}, s32[512]{0:T(512)S(1)}, u32[]{:S(2)}, u32[]{:S(2)}) collective-permute-start(s32[512]{0:T(512)S(1)} %get-tuple-element.426), channel_id=1, source_target_pairs={{0,8},{8,16},{16,24},{24,32},{32,40},{40,48},{48,56},{56,64},{64,7... | collective-permute-start | bytes 6152 | tf_op jit(solution)/shard_map/while/body/eval_jaxpr/ppermute | solution.py:12
  589.3 17.6 %collective-permute-start.1 = (bf16[512,1024]{1,0:T(8,128)(2,1)S(1)}, bf16[512,1024]{1,0:T(8,128)(2,1)S(1)}, u32[]{:S(2)}, u32[]{:S(2)}) collective-permute-start(bf16[512,1024]{1,0:T(8,128)(2,1)S(1)} %get-tuple-element.425), channel_id=1, source_target_pairs={{0,8},{8,16},{16,24},{24,32},{32,40},{40,48},{48,56},{56,64},{64,7... | collective-permute-start | bytes 3145736 | tf_op jit(solution)/shard_map/while/body/eval_jaxpr/ppermute | solution.py:12
  607.9 17.6 %collective-permute-start.1 = (bf16[512,1024]{1,0:T(8,128)(2,1)S(1)}, bf16[512,1024]{1,0:T(8,128)(2,1)S(1)}, u32[]{:S(2)}, u32[]{:S(2)}) collective-permute-start(bf16[512,1024]{1,0:T(8,128)(2,1)S(1)} %get-tuple-element.425), channel_id=1, source_target_pairs={{0,8},{8,16},{16,24},{24,32},{32,40},{40,48},{48,56},{56,64},{64,7... | collective-permute-start | bytes 3145736 | tf_op jit(solution)/shard_map/while/body/eval_jaxpr/ppermute | solution.py:12
  608.0 17.6 %collective-permute-start = (s32[512]{0:T(512)S(1)}, s32[512]{0:T(512)S(1)}, u32[]{:S(2)}, u32[]{:S(2)}) collective-permute-start(s32[512]{0:T(512)S(1)} %get-tuple-element.426), channel_id=1, source_target_pairs={{0,8},{8,16},{16,24},{24,32},{32,40},{40,48},{48,56},{56,64},{64,7... | collective-permute-start | bytes 6152 | tf_op jit(solution)/shard_map/while/body/eval_jaxpr/ppermute | solution.py:12
  (22 other events, 309.8 us)
where the time goes:
time: 640 us; the launch traced here: 639 us
  waiting for transfers between devices  570 us (89%)
  matrix products  27.8 us (4%)
  starting transfers between devices  24.8 us (4%)
  other arithmetic  7.69 us (1%)
  local copies, waits for them, and re-layouts  6.9 us (1%)
    ppermute x62, waiting for transfers between devices, passed_along(): return lax.ppermute(value, axis, pairs)  535 us
    dot_general x32, matrix products, compare(): lax.dot_general(panel_units, key_units, (((1,), (1,)), ((), ())), preferr...  27.8 us
    all_to_all x1, waiting for transfers between devices, on_device(): lax.all_to_all(send_units, 'own', split_axis=0, concat_axis=0, tiled=True)  25 us
  transfers between devices with their start and end apart: 65, of which 34 were waited for; matrix products, arithmetic and copies ran while one was open for 1% of the time, Pallas kernels for 0%

commit v1 on v0

v1 whole, which is shorter than its diff:
```python
import functools

import jax
import jax.numpy as jnp
from jax import lax
from jax.experimental import pallas as pl
from jax.experimental.pallas import tpu as pltpu
from jax.sharding import PartitionSpec as P


TILE = 32
GROUP = 8
ROWS = TILE * GROUP
CHUNK = 2 * ROWS

TREE = (
    (1, (0, 0), (1, 0)),
    (1, (0, 0), (-1, 0)),
    (1, (0, 0), (0, 1)),
    (1, (0, 0), (0, -1)),
    (2, (0, 1), (1, 0)),
    (2, (0, -1), (-1, 0)),
    (2, (-1, 0), (0, 1)),
    (2, (1, 0), (0, -1)),
    (3, (1, 0), (1, 0)),
    (3, (-1, -1), (-1, 0)),
    (3, (0, 1), (0, 1)),
    (3, (1, -1), (0, -1)),
    (4, (1, 1), (1, 0)),
    (4, (-1, 1), (0, 1)),
    (4, (2, 3), (0, -1)),
)
SIDE = 4
OWNERS = 8
CLUSTERS = 4


def wrap(node):
    return (node[0] % SIDE, node[1] % SIDE)


def plane_pairs(dx, dy, flip):
    pairs = []
    for y in range(SIDE):
        for x in range(SIDE):
            for core in range(2):
                source = (y * SIDE + x) * 2 + core
                dest = (((y + dy) % SIDE) * SIDE + (x + dx) % SIDE) * 2 + (core ^ flip)
                pairs.append((source, dest))
    return pairs


def in_plane(value, dx, dy):
    return lax.ppermute(value, "grp", plane_pairs(dx, dy, 0))


def other_core(value):
    return lax.ppermute(value, "grp", plane_pairs(0, 0, 1))


def along(value, step, count):
    return lax.ppermute(value, "own", [(i, (i + step) % count) for i in range(count)])


def unit_rows(values):
    wide = values.astype(jnp.float32)
    return (wide * lax.rsqrt(jnp.sum(wide * wide, axis=-1, keepdims=True) + 1e-06)).astype(
        jnp.bfloat16
    )


def compare_kernel(queries, keys, with_self, with_prev, where_ref, pattern_ref, *refs):
    n_ops = max([h for _, h, _ in queries] + [k[0] for k in keys]) + 1
    arrays = refs[:n_ops]
    refs = refs[n_ops:]
    if with_prev:
        prev_ref, refs = refs[0], refs[1:]
    out_ref, q_pan, k_pan, q_col, k_col, acc, spread, meta, own_vec = refs[:9]
    own_s, q_base, k_base, q_next, k_next, q_order, q_own_s, k_place, q_place, sems = refs[9:19]
    if with_self:
        q_self, k_self = refs[19:21]
    n_q, n_k = len(queries), len(keys)
    k_tiles = n_k * GROUP
    per = CHUNK // TILE
    group, depth = where_ref[0], where_ref[1]
    chip_y, chip_x, core = group // (2 * SIDE), (group // 2) % SIDE, group % 2

    for i in range(n_q + n_k):
        if i < n_q:
            low, high, _ = queries[i]
            row = ROWS if low == high else ROWS // 2
        else:
            high, row = keys[i - n_q][0], ROWS
        pltpu.make_async_copy(
            arrays[high].at[pl.ds(row, 8), pl.ds(0, ROWS)], meta.at[i], sems.at[0]
        ).start()
    pltpu.make_async_copy(meta, meta, sems.at[0]).wait()
    for i in range(n_q + n_k):
        own_vec[i : i + 1, :] = meta[i].astype(jnp.float32)[1:2, :].astype(jnp.int32)
    to_scalar = pltpu.make_async_copy(own_vec, own_s, sems.at[0])
    to_scalar.start()
    to_scalar.wait()

    for o in range(OWNERS + 1):
        q_next[o] = 0
        k_next[o] = 0

    def count(i, table):
        for j in range(GROUP):
            o = own_s[i, j * TILE]
            table[o] = table[o] + 1

    def count_q(i, carry):
        count(i, q_next)
        return carry

    def count_k(i, carry):
        count(i, k_next)
        return carry

    lax.fori_loop(0, n_q, count_q, 0)
    lax.fori_loop(n_q, n_q + n_k, count_k, 0)
    for base, table in ((q_base, q_next), (k_base, k_next)):
        total = jnp.int32(0)
        for o in range(OWNERS + 1):
            here = table[o]
            base[o] = total
            table[o] = total
            total = total + here

    for i in range(n_q):
        low, high, _ = queries[i]
        for first, ref, shift in ((0, low, 0), (GROUP // 2, high, 0 if low == high else GROUP // 2)):

            def put_q(j, carry, i=i, ref=ref, shift=shift):
                o = own_s[i, j * TILE]
                to = q_next[o]
                q_next[o] = to + 1
                q_order[to] = i * GROUP + j
                q_own_s[to] = o
                q_place[i * GROUP + j] = to
                pltpu.make_async_copy(
                    arrays[ref].at[pl.ds(pl.multiple_of((j - shift) * TILE, TILE), TILE)],
                    q_pan.at[pl.ds(pl.multiple_of(to * TILE, TILE), TILE)],
                    sems.at[1],
                ).start()
                return carry

            lax.fori_loop(first, first + GROUP // 2, put_q, 0, unroll=True)
    for i in range(n_k):
        src = arrays[keys[i][0]]

        def put_k(j, carry, i=i, src=src):
            o = own_s[n_q + i, j * TILE]
            to = k_next[o]
            k_next[o] = to + 1
            k_place[i * GROUP + j] = to
            pltpu.make_async_copy(
                src.at[pl.ds(pl.multiple_of(j * TILE, TILE), TILE), pl.ds(0, src.shape[1])],
                k_pan.at[pl.ds(pl.multiple_of(to * TILE, TILE), TILE)],
                sems.at[2],
            ).start()
            return carry

        lax.fori_loop(0, GROUP, put_k, 0, unroll=True)

    def column(row):
        return jnp.transpose(jnp.broadcast_to(row, (128, ROWS)))

    def spread_column(col, place, i, panel):
        for j in range(GROUP):
            to = pl.multiple_of(place[i * GROUP + j] * TILE, TILE)
            panel[pl.ds(to, TILE), :] = col[j * TILE : (j + 1) * TILE, :]

    def label(i):
        info = meta[i].astype(jnp.float32)
        return info[1:2, :] * CLUSTERS + info[0:1, :]

    for i in range(n_q):
        spread_column(column(label(i)), q_place, i, q_col)
    for i in range(n_k):
        _, dx, dy, flip = keys[i]
        source = (((chip_y - dy) % SIDE) * SIDE + (chip_x - dx) % SIDE) * 2 + (core + flip) % 2
        allowed = pattern_ref[group, source] > 0
        spread_column(column(jnp.where(allowed, label(n_q + i), -1.0)), k_place, i, k_col)
    if with_self:
        q_self[...] = jnp.full_like(q_self, -1.0)
        k_self[...] = jnp.full_like(k_self, -2.0)
        names = lax.broadcasted_iota(jnp.int32, (ROWS, 128), 0).astype(jnp.float32)
        spread_column(names, q_place, 0, q_self)
        spread_column(names, k_place, 0, k_self)
    pltpu.make_async_copy(q_pan, q_pan, sems.at[1]).wait()
    pltpu.make_async_copy(k_pan, k_pan, sems.at[2]).wait()

    def block_step(b, carry):
        rows = pl.ds(pl.multiple_of(b * ROWS, ROWS), ROWS)
        q_row = jnp.transpose(q_col[rows, :])[0:1, :]
        if with_self:
            q_name = jnp.transpose(q_self[rows, :])[0:1, :]
        acc[...] = jnp.full_like(acc, -1.0)
        lo = k_base[q_own_s[b * GROUP]]
        hi = k_base[q_own_s[b * GROUP + GROUP - 1] + 1]

        def chunk_step(m, inner):
            at = pl.multiple_of(jnp.minimum(lo + m * per, k_tiles - per) * TILE, TILE)
            span = pl.ds(at, CHUNK)
            scores = lax.dot_general(
                k_pan[span, :], q_pan[rows, :], (((1,), (1,)), ((), ())),
                preferred_element_type=jnp.float32,
            )
            col = k_col[span, :]
            if with_self:
                name = k_self[span, :]
            for h in range(ROWS // 128):
                lanes = slice(h * 128, (h + 1) * 128)
                match = col == q_row[:, lanes]
                if with_self:
                    match = match & (name != q_name[:, lanes])
                found = jnp.where(match, scores[:, lanes], -1.0)
                found = jnp.max(found.reshape(CHUNK // 8, 8, 128), axis=0)
                acc[:, lanes] = jnp.maximum(acc[:, lanes], found)
            return inner

        lax.fori_loop(0, (hi - lo + per - 1) // per, chunk_step, 0)
        done = column(jnp.max(acc[...], axis=0, keepdims=True))
        for j in range(GROUP):
            to = pl.multiple_of(q_order[b * GROUP + j] * TILE, TILE)
            spread[pl.ds(to, TILE), :] = done[j * TILE : (j + 1) * TILE, :]
        return carry

    lax.fori_loop(0, n_q, block_step, 0)
    for s in range(n_q):
        row = jnp.transpose(spread[s * ROWS : (s + 1) * ROWS, :])[0:1, :]
        to = (depth - queries[s][2] + 2 * n_q) % n_q
        if with_prev:
            row = jnp.maximum(row, prev_ref[to])
        out_ref[to] = row


def compare(where, pattern, arrays, queries, keys, with_self, prev=None):
    n_q, n_k = len(queries), len(keys)
    width = arrays[0].shape[1]
    smem = pl.BlockSpec(memory_space=pltpu.SMEM)
    vmem = pl.BlockSpec(memory_space=pltpu.VMEM)
    anywhere = pl.BlockSpec(memory_space=pl.ANY)
    slots = -(-(n_q + n_k) // 8) * 8
    scratch = [
        pltpu.VMEM((n_q * ROWS, width), jnp.bfloat16),
        pltpu.VMEM((n_k * ROWS, width), jnp.bfloat16),
        pltpu.VMEM((n_q * ROWS, 128), jnp.float32),
        pltpu.VMEM((n_k * ROWS, 128), jnp.float32),
        pltpu.VMEM((8, ROWS), jnp.float32),
        pltpu.VMEM((n_q * ROWS, 128), jnp.float32),
        pltpu.VMEM((n_q + n_k, 8, ROWS), jnp.bfloat16),
        pltpu.VMEM((slots, ROWS), jnp.int32),
        pltpu.SMEM((slots, ROWS), jnp.int32),
        pltpu.SMEM((OWNERS + 1,), jnp.int32),
        pltpu.SMEM((OWNERS + 1,), jnp.int32),
        pltpu.SMEM((OWNERS + 1,), jnp.int32),
        pltpu.SMEM((OWNERS + 1,), jnp.int32),
        pltpu.SMEM((n_q * GROUP,), jnp.int32),
        pltpu.SMEM((n_q * GROUP,), jnp.int32),
        pltpu.SMEM((n_k * GROUP,), jnp.int32),
        pltpu.SMEM((n_q * GROUP,), jnp.int32),
        pltpu.SemaphoreType.DMA((3,)),
    ]
    if with_self:
        scratch += [
            pltpu.VMEM((n_q * ROWS, 128), jnp.float32),
            pltpu.VMEM((n_k * ROWS, 128), jnp.float32),
        ]
    extra = () if prev is None else (prev,)
    return pl.pallas_call(
        functools.partial(compare_kernel, queries, keys, with_self, prev is not None),
        out_shape=jax.ShapeDtypeStruct((n_q, 1, ROWS), jnp.float32),
        in_specs=[smem] * 2 + [anywhere] * len(arrays) + [vmem] * len(extra),
        out_specs=vmem,
        scratch_shapes=scratch,
        cost_estimate=pl.CostEstimate(
            flops=2 * n_q * n_k * ROWS * ROWS * width // 3,
            bytes_accessed=(n_q + n_k) * ROWS * width * 2,
            transcendentals=0,
        ),
        name="compare",
    )(where, pattern, *arrays, *extra)


def search(embeddings, cluster_ids, owners, pattern):
    n_own = lax.axis_size("own")
    tiles_here, tile_rows, width = embeddings.shape
    where = jnp.stack([lax.axis_index("grp"), lax.axis_index("own")]).astype(jnp.int32)

    labels = jnp.stack([cluster_ids, jnp.broadcast_to(owners, cluster_ids.shape)])
    labels = labels.reshape(2, ROWS).astype(jnp.bfloat16)
    labels = jnp.pad(labels, ((0, 6), (0, width - ROWS)))
    shard = jnp.concatenate([unit_rows(embeddings).reshape(ROWS, width), labels], axis=0)

    up, down = [shard], [shard]
    line = [shard]
    queries = [(0, 0, 0)]
    for hop in range(1, n_own // 2):
        up.append(along(up[-1], 1, n_own))
        down.append(along(down[-1], -1, n_own))
        queries += [(len(line), len(line), hop), (len(line) + 1, len(line) + 1, -hop)]
        line += [up[-1], down[-1]]
    far_low = along(up[-1][: ROWS // 2], 1, n_own)
    far_high = along(down[-1][ROWS // 2 :], -1, n_own)
    queries.append((len(line), len(line) + 1, n_own // 2))
    line += [far_low, far_high]

    held = {(0, 0): shard}
    swapped = {(0, 0): other_core(shard)}
    nodes = {1: [(0, 0)], 2: []}
    for turn, source, (dx, dy) in TREE:
        node = wrap((source[0] + dx, source[1] + dy))
        held[node] = in_plane(held[wrap(source)], dx, dy)
        swapped[node] = other_core(held[node])
        nodes[1 if turn < 4 else 2].append(node)

    best = None
    for call in (1, 2):
        arrays, keys = list(line), []
        for dx, dy in nodes[call]:
            for flip, table in enumerate((held, swapped)):
                if (dx, dy, flip) == (0, 0, 0):
                    keys.append((0, 0, 0, 0))
                else:
                    keys.append((len(arrays), dx, dy, flip))
                    arrays.append(table[(dx, dy)])
        best = compare(where, pattern, arrays, queries, keys, call == 1, best)

    returned = lax.all_to_all(best, "own", split_axis=0, concat_axis=0, tiled=True)
    return jnp.max(returned, axis=0).reshape(tiles_here, tile_rows)


def solution(mesh):
    placed = (P(("grp", "own"), None, None), P(("grp", "own"), None), P(("grp", "own"), None), P())
    return jax.shard_map(
        search, mesh=mesh, in_specs=placed, out_specs=P(("grp", "own"), None), check_vma=False
    )
```

time: 640 us -> 166 us (0.26)
  waiting for transfers between devices: 570 us -> 65.7 us
  Pallas kernels: 0 us -> 40.7 us
  matrix products: 27.8 us -> 0 us
  blocking collectives: 0 us -> 12.5 us
  starting transfers between devices: 24.8 us -> 37.3 us
    ppermute x62 -> x39, waiting for transfers between devices: 535 us -> 65.7 us  [the longest x15 37.5 us: in_plane(): return lax.ppermute(value, 'grp', plane_pairs(dx, dy, 0))]
    pallas_call x0 -> x2, Pallas kernels: none -> 40.7 us  [compare(): pl.pallas_call(functools.partial(compare_kernel, queries, keys, with_self...]
    all_to_all x3 -> x0, waiting for transfers between devices: 34.5 us -> none  [the longest x1 25 us: on_device(): lax.all_to_all(send_units, 'own', split_axis=0, concat_axis=0, tiled=True)]
    ppermute x62 -> x39, starting transfers between devices: 6.66 us -> 37.3 us  [the longest x15 23.8 us: in_plane(): return lax.ppermute(value, 'grp', plane_pairs(dx, dy, 0))]
    dot_general x32 -> x0, matrix products: 27.8 us -> none  [compare(): lax.dot_general(panel_units, key_units, (((1,), (1,)), ((), ())), preferr...]
    all_to_all x3 -> x0, starting transfers between devices: 18.2 us -> none  [the longest x1 8.57 us: on_device(): lax.all_to_all(send_ids, 'own', split_axis=0, concat_axis=0, tiled=True)]
    all_to_all x0 -> x1, blocking collectives: none -> 12.5 us  [search(): lax.all_to_all(best, 'own', split_axis=0, concat_axis=0, tiled=True)]
  transfers between devices with their start and end apart: 65 -> 39, of which waited for: 34 -> 14; matrix products, arithmetic and copies ran while one was open for 1% -> 0% of each run, Pallas kernels for 0% -> 16%
where the time goes in v1:
time: 166 us; the launch traced here: 163 us
  waiting for transfers between devices  65.7 us (40%)
  Pallas kernels  40.7 us (25%)
  starting transfers between devices  37.3 us (22%)
  blocking collectives  12.5 us (8%)
  local copies, waits for them, and re-layouts  3.98 us (2%)
  other arithmetic  2.12 us (1%)
    pallas_call x2, Pallas kernels, compare(): pl.pallas_call(functools.partial(compare_kernel, queries, keys, with_self...  40.7 us
    ppermute x15, waiting for transfers between devices, in_plane(): return lax.ppermute(value, 'grp', plane_pairs(dx, dy, 0))  37.5 us
    ppermute x8, waiting for transfers between devices, along(): lax.ppermute(value, 'own', [(i, (i + step) % count) for i in range(count)])  27.3 us
    ppermute x15, starting transfers between devices, in_plane(): return lax.ppermute(value, 'grp', plane_pairs(dx, dy, 0))  23.8 us
    all_to_all x1, blocking collectives, search(): lax.all_to_all(best, 'own', split_axis=0, concat_axis=0, tiled=True)  12.5 us
    ppermute x8, starting transfers between devices, along(): lax.ppermute(value, 'own', [(i, (i + step) % count) for i in range(count)])  11.8 us
  transfers between devices with their start and end apart: 39, of which 14 were waited for; matrix products, arithmetic and copies ran while one was open for 0% of the time, Pallas kernels for 16%

profile of v1, /device:TPU:32, one launch (start us, length us, event | category | flops | bytes accessed | tf_op | source)
XLA Modules:
  0.0 162.8 jit_solution(3319563673866528648)
XLA Ops:
  0.0 1.3 fusion
  1.3 0.2 fusion.1
  1.5 0.5 copy-done.34
  2.3 1.9 %collective-permute-start.1 = (bf16[264,1024]{1,0:T(8,128)(2,1)S(1)}, bf16[264,1024]{1,0:T(8,128)(2,1)S(1)}, u32[]{:S(2)}, u32[]{:S(2)}) collective-permute-start(bf16[264,1024]{1,0:T(8,128)(2,1)S(1)} %pad_maximum_fusion.refs_0_), channel_id=1, source_target_pairs={{0,7},{1,0},{2,1},{3,2},{4,3},{5,4},{6,5},{7,6},{8,15},{9,8},{10,9... | collective-permute-start | bytes 1622024 | tf_op jit(solution)/shard_map/ppermute | solution.py:62
  4.2 0.2 collective-permute-start
  4.4 3.0 %collective-permute-start.16 = (bf16[264,1024]{1,0:T(8,128)(2,1)S(1)}, bf16[264,1024]{1,0:T(8,128)(2,1)S(1)}, u32[]{:S(2)}, u32[]{:S(2)}) collective-permute-start(bf16[264,1024]{1,0:T(8,128)(2,1)S(1)} %pad_maximum_fusion.refs_0_), channel_id=1, source_target_pairs={{0,192},{8,200},{16,208},{24,216},{32,224},{40,232},{48,240},{56,2... | collective-permute-start | bytes 1622024 | tf_op jit(solution)/shard_map/ppermute | solution.py:54
  7.4 1.5 collective-permute-start.22
  8.9 7.7 %collective-permute-done.1.refs_2_ = bf16[264,1024]{1,0:T(8,128)(2,1)S(1)} collective-permute-done((bf16[264,1024]{1,0:T(8,128)(2,1)S(1)}, bf16[264,1024]{1,0:T(8,128)(2,1)S(1)}, u32[]{:S(2)}, u32[]{:S(2)}) %collective-permute-start.1) | collective-permute-done | bytes 540704 | tf_op jit(solution)/shard_map/ppermute | solution.py:62
  16.6 2.8 %collective-permute-start.12 = (bf16[264,1024]{1,0:T(8,128)(2,1)S(1)}, bf16[264,1024]{1,0:T(8,128)(2,1)S(1)}, u32[]{:S(2)}, u32[]{:S(2)}) collective-permute-start(bf16[264,1024]{1,0:T(8,128)(2,1)S(1)} %pad_maximum_fusion.refs_0_), channel_id=1, source_target_pairs={{0,48},{8,56},{16,0},{24,8},{32,16},{40,24},{48,32},{56,40},{64,11... | collective-permute-start | bytes 1622024 | tf_op jit(solution)/shard_map/ppermute | solution.py:54
  19.3 1.0 collective-permute-done.refs_1_
  20.3 3.0 %collective-permute-start.3 = (bf16[264,1024]{1,0:T(8,128)(2,1)S(1)}, bf16[264,1024]{1,0:T(8,128)(2,1)S(1)}, u32[]{:S(2)}, u32[]{:S(2)}) collective-permute-start(bf16[264,1024]{1,0:T(8,128)(2,1)S(1)} %collective-permute-done.1.refs_2_), channel_id=1, source_target_pairs={{0,7},{1,0},{2,1},{3,2},{4,3},{5,4},{6,5},{7,6},{8,15},{9,8},{10,9... | collective-permute-start | bytes 1622024 | tf_op jit(solution)/shard_map/ppermute | solution.py:62
  23.4 0.6 collective-permute-start.2
  24.0 2.3 %collective-permute-start.17 = (bf16[264,1024]{1,0:T(8,128)(2,1)S(1)}, bf16[264,1024]{1,0:T(8,128)(2,1)S(1)}, u32[]{:S(2)}, u32[]{:S(2)}) collective-permute-start(bf16[264,1024]{1,0:T(8,128)(2,1)S(1)} %collective-permute-done.16.refs_16_), channel_id=1, source_target_pairs={{0,48},{8,56},{16,0},{24,8},{32,16},{40,24},{48,32},{56,40},{64,11... | collective-permute-start | bytes 1622024 | tf_op jit(solution)/shard_map/ppermute | solution.py:54
  26.2 5.7 %collective-permute-done.12.refs_12_ = bf16[264,1024]{1,0:T(8,128)(2,1)S(1)} collective-permute-done((bf16[264,1024]{1,0:T(8,128)(2,1)S(1)}, bf16[264,1024]{1,0:T(8,128)(2,1)S(1)}, u32[]{:S(2)}, u32[]{:S(2)}) %collective-permute-start.12) | collective-permute-done | bytes 540704 | tf_op jit(solution)/shard_map/ppermute | solution.py:54
  32.0 3.0 %collective-permute-start.30 = (bf16[264,1024]{1,0:T(8,128)(2,1)S(1)}, bf16[264,1024]{1,0:T(8,128)(2,1)S(1)}, u32[]{:S(2)}, u32[]{:S(2)}) collective-permute-start(bf16[264,1024]{1,0:T(8,128)(2,1)S(1)} %collective-permute-done.22.refs_10_), channel_id=1, source_target_pairs={{0,192},{8,200},{16,208},{24,216},{32,224},{40,232},{48,240},{56,2... | collective-permute-start | bytes 1622024 | tf_op jit(solution)/shard_map/ppermute | solution.py:54
  35.0 1.2 collective-permute-start.9
  36.2 0.8 collective-permute-start.13
  37.1 1.9 %collective-permute-done.2.refs_3_ = bf16[264,1024]{1,0:T(8,128)(2,1)S(1)} collective-permute-done((bf16[264,1024]{1,0:T(8,128)(2,1)S(1)}, bf16[264,1024]{1,0:T(8,128)(2,1)S(1)}, u32[]{:S(2)}, u32[]{:S(2)}) %collective-permute-start.2) | collective-permute-done | bytes 540704 | tf_op jit(solution)/shard_map/ppermute | solution.py:62
  39.0 0.2 collective-permute-start.32
  39.2 2.6 %collective-permute-done.17.refs_20_ = bf16[264,1024]{1,0:T(8,128)(2,1)S(1)} collective-permute-done((bf16[264,1024]{1,0:T(8,128)(2,1)S(1)}, bf16[264,1024]{1,0:T(8,128)(2,1)S(1)}, u32[]{:S(2)}, u32[]{:S(2)}) %collective-permute-start.17) | collective-permute-done | bytes 540704 | tf_op jit(solution)/shard_map/ppermute | solution.py:54
  41.8 1.6 collective-permute-start.35
  43.3 8.5 %collective-permute-done.9.refs_18_ = bf16[264,1024]{1,0:T(8,128)(2,1)S(1)} collective-permute-done((bf16[264,1024]{1,0:T(8,128)(2,1)S(1)}, bf16[264,1024]{1,0:T(8,128)(2,1)S(1)}, u32[]{:S(2)}, u32[]{:S(2)}) %collective-permute-start.9) | collective-permute-done | bytes 540704 | tf_op jit(solution)/shard_map/ppermute | solution.py:54
  51.8 0.8 collective-permute-done.13.refs_22_
  52.6 6.3 %collective-permute-done.32.refs_26_ = bf16[264,1024]{1,0:T(8,128)(2,1)S(1)} collective-permute-done((bf16[264,1024]{1,0:T(8,128)(2,1)S(1)}, bf16[264,1024]{1,0:T(8,128)(2,1)S(1)}, u32[]{:S(2)}, u32[]{:S(2)}) %collective-permute-start.32) | collective-permute-done | bytes 540704 | tf_op jit(solution)/shard_map/ppermute | solution.py:54
  58.9 3.2 %collective-permute-done.35.refs_30_ = bf16[264,1024]{1,0:T(8,128)(2,1)S(1)} collective-permute-done((bf16[264,1024]{1,0:T(8,128)(2,1)S(1)}, bf16[264,1024]{1,0:T(8,128)(2,1)S(1)}, u32[]{:S(2)}, u32[]{:S(2)}) %collective-permute-start.35) | collective-permute-done | bytes 540704 | tf_op jit(solution)/shard_map/ppermute | solution.py:54
  62.1 3.0 %collective-permute-start.5 = (bf16[264,1024]{1,0:T(8,128)(2,1)S(1)}, bf16[264,1024]{1,0:T(8,128)(2,1)S(1)}, u32[]{:S(2)}, u32[]{:S(2)}) collective-permute-start(bf16[264,1024]{1,0:T(8,128)(2,1)S(1)} %collective-permute-done.3.refs_4_), channel_id=1, source_target_pairs={{0,7},{1,0},{2,1},{3,2},{4,3},{5,4},{6,5},{7,6},{8,15},{9,8},{10,9... | collective-permute-start | bytes 1622024 | tf_op jit(solution)/shard_map/ppermute | solution.py:62
  65.2 2.3 %collective-permute-start.18 = (bf16[264,1024]{1,0:T(8,128)(2,1)S(1)}, bf16[264,1024]{1,0:T(8,128)(2,1)}, u32[]{:S(2)}, u32[]{:S(2)}) collective-permute-start(bf16[264,1024]{1,0:T(8,128)(2,1)S(1)} %collective-permute-done.17.refs_20_), channel_id=1, source_target_pairs={{0,48},{8,56},{16,0},{24,8},{32,16},{40,24},{48,32},{56,40},{64,11... | collective-permute-start | bytes 1622024 | tf_op jit(solution)/shard_map/ppermute | solution.py:54
  67.4 1.7 %collective-permute-start.37 = (bf16[264,1024]{1,0:T(8,128)(2,1)S(1)}, bf16[264,1024]{1,0:T(8,128)(2,1)}, u32[]{:S(2)}, u32[]{:S(2)}) collective-permute-start(bf16[264,1024]{1,0:T(8,128)(2,1)S(1)} %collective-permute-done.30.refs_24_), channel_id=1, source_target_pairs={{0,192},{8,200},{16,208},{24,216},{32,224},{40,232},{48,240},{56,2... | collective-permute-start | bytes 1622024 | tf_op jit(solution)/shard_map/ppermute | solution.py:54
  69.2 5.7 %collective-permute-done.5.refs_6_ = bf16[264,1024]{1,0:T(8,128)(2,1)S(1)} collective-permute-done((bf16[264,1024]{1,0:T(8,128)(2,1)S(1)}, bf16[264,1024]{1,0:T(8,128)(2,1)S(1)}, u32[]{:S(2)}, u32[]{:S(2)}) %collective-permute-start.5) | collective-permute-done | bytes 540704 | tf_op jit(solution)/shard_map/ppermute | solution.py:62
  74.9 3.9 %collective-permute-done.4.refs_5_ = bf16[264,1024]{1,0:T(8,128)(2,1)S(1)} collective-permute-done((bf16[264,1024]{1,0:T(8,128)(2,1)S(1)}, bf16[264,1024]{1,0:T(8,128)(2,1)S(1)}, u32[]{:S(2)}, u32[]{:S(2)}) %collective-permute-start.4) | collective-permute-done | bytes 540704 | tf_op jit(solution)/shard_map/ppermute | solution.py:62
  78.8 0.5 collective-permute-start.29
  79.4 0.4 collective-permute-start.36
  79.8 0.9 collective-permute-done.28.refs_21_
  80.7 1.2 collective-permute-start.14
  81.9 2.2 %collective-permute-start.19 = (bf16[264,1024]{1,0:T(8,128)(2,1)}, bf16[264,1024]{1,0:T(8,128)(2,1)}, u32[]{:S(2)}, u32[]{:S(2)}) collective-permute-start(bf16[264,1024]{1,0:T(8,128)(2,1)} %collective-permute-done.18.refs_28_), channel_id=1, source_target_pairs={{0,192},{8,200},{16,208},{24,216},{32,224},{40,232},{48,240},{56,2... | collective-permute-start | bytes 1622024 | tf_op jit(solution)/shard_map/ppermute | solution.py:54
  84.4 0.6 copy-done.28
  85.0 10.4 %collective-permute-done.10.refs_9_ = bf16[264,1024]{1,0:T(8,128)(2,1)} collective-permute-done((bf16[264,1024]{1,0:T(8,128)(2,1)S(1)}, bf16[264,1024]{1,0:T(8,128)(2,1)}, u32[]{:S(2)}, u32[]{:S(2)}) %collective-permute-start.10) | collective-permute-done | bytes 540704 | tf_op jit(solution)/shard_map/ppermute | solution.py:54
  95.4 3.0 %collective-permute-start.7 = (bf16[136,1024]{1,0:T(8,128)(2,1)S(1)}, bf16[136,1024]{1,0:T(8,128)(2,1)S(1)}, u32[]{:S(2)}, u32[]{:S(2)}) collective-permute-start(bf16[136,1024]{1,0:T(8,128)(2,1)S(1)} %slice.9), channel_id=1, source_target_pairs={{0,7},{1,0},{2,1},{3,2},{4,3},{5,4},{6,5},{7,6},{8,15},{9,8},{10,9... | collective-permute-start | bytes 835592 | tf_op jit(solution)/shard_map/ppermute | solution.py:62
  98.5 0.6 pad_add_fusion.where_ref
  99.1 7.2 %collective-permute-done.6.refs_7_ = bf16[128,1024]{1,0:T(8,128)(2,1)} collective-permute-done((bf16[128,1024]{1,0:T(8,128)(2,1)S(1)}, bf16[128,1024]{1,0:T(8,128)(2,1)}, u32[]{:S(2)}, u32[]{:S(2)}) %collective-permute-start.6) | collective-permute-done | bytes 262176 | tf_op jit(solution)/shard_map/ppermute | solution.py:62
  106.3 0.5 collective-permute-start.15
  107.0 26.8 %compare.37.refs_15_ = f32[8,1,256]{2,1,0:T(1,128)} custom-call(s32[2]{0:T(128)} %pad_add_fusion.where_ref, s32[32,32]{1,0:T(8,128)} %pattern_ref.3, bf16[264,1024]{1,0:T(8,128)(2,1)} %copy-done.1, bf16[264,1024]{1,0:T(8,128)(2,1)} %copy-done.6, bf16[264,1024]{1,0:T(8,128)(2,1)} %copy-done.5, bf16[264,1024]{1,0:T(8,128)(2,1)} %copy-done.8, ...), custom_call_target="tpu_custom_call" | custom-call | flops 9305762816 | bytes 17825792 | tf_op jit(solution)/shard_map/compare/pallas_call | solution.py:273
  133.8 0.8 copy-done.30
  134.6 0.2 copy-done.31
  134.8 0.8 copy-done.32
  135.6 14.0 %compare.38 = f32[8,1,256]{2,1,0:T(1,128)} custom-call(s32[2]{0:T(128)} %pad_add_fusion.where_ref, s32[32,32]{1,0:T(8,128)} %pattern_ref.3, bf16[264,1024]{1,0:T(8,128)(2,1)} %copy-done.1, bf16[264,1024]{1,0:T(8,128)(2,1)} %copy-done.6, bf16[264,1024]{1,0:T(8,128)(2,1)} %copy-done.5, bf16[264,1024]{1,0:T(8,128)(2,1)} %copy-done.8, ...), custom_call_target="tpu_custom_call" | custom-call | flops 2147483648 | bytes 7340032 | tf_op jit(solution)/shard_map/compare/pallas_call | solution.py:273
  149.6 12.5 %all_to_all.5 = f32[8,1,256]{2,1,0:T(1,128)S(1)} all-to-all(f32[8,1,256]{2,1,0:T(1,128)} %compare.38), channel_id=1, replica_groups=mesh['grp'=32,'own'=8] {'own'}, dimensions={0} | all-to-all | bytes 16384 | tf_op jit(solution)/shard_map/all_to_all | solution.py:332
  162.2 0.7 reshape.28
  (118 shorter events, 0.9 us)
Async XLA Ops:
  2.3 96.2 %copy-start.1 = (bf16[264,1024]{1,0:T(8,128)(2,1)}, bf16[264,1024]{1,0:T(8,128)(2,1)S(1)}, u32[]{:S(2)}) copy-start(bf16[264,1024]{1,0:T(8,128)(2,1)S(1)} %pad_maximum_fusion.refs_0_) | copy-start | bytes 1622020
  2.3 14.3 %collective-permute-start.1 = (bf16[264,1024]{1,0:T(8,128)(2,1)S(1)}, bf16[264,1024]{1,0:T(8,128)(2,1)S(1)}, u32[]{:S(2)}, u32[]{:S(2)}) collective-permute-start(bf16[264,1024]{1,0:T(8,128)(2,1)S(1)} %pad_maximum_fusion.refs_0_), channel_id=1, source_target_pairs={{0,7},{1,0},{2,1},{3,2},{4,3},{5,4},{6,5},{7,6},{8,15},{9,8},{10,9... | collective-permute-start | bytes 1622024 | tf_op jit(solution)/shard_map/ppermute | solution.py:62
  4.2 16.1 %collective-permute-start = (bf16[264,1024]{1,0:T(8,128)(2,1)S(1)}, bf16[264,1024]{1,0:T(8,128)(2,1)S(1)}, u32[]{:S(2)}, u32[]{:S(2)}) collective-permute-start(bf16[264,1024]{1,0:T(8,128)(2,1)S(1)} %pad_maximum_fusion.refs_0_), channel_id=1, source_target_pairs={{0,1},{1,2},{2,3},{3,4},{4,5},{5,6},{6,7},{7,0},{8,9},{9,10},{10,1... | collective-permute-start | bytes 1622024 | tf_op jit(solution)/shard_map/ppermute | solution.py:62
  4.4 15.9 %collective-permute-start.16 = (bf16[264,1024]{1,0:T(8,128)(2,1)S(1)}, bf16[264,1024]{1,0:T(8,128)(2,1)S(1)}, u32[]{:S(2)}, u32[]{:S(2)}) collective-permute-start(bf16[264,1024]{1,0:T(8,128)(2,1)S(1)} %pad_maximum_fusion.refs_0_), channel_id=1, source_target_pairs={{0,192},{8,200},{16,208},{24,216},{32,224},{40,232},{48,240},{56,2... | collective-permute-start | bytes 1622024 | tf_op jit(solution)/shard_map/ppermute | solution.py:54
  7.4 16.0 %collective-permute-start.22 = (bf16[264,1024]{1,0:T(8,128)(2,1)S(1)}, bf16[264,1024]{1,0:T(8,128)(2,1)S(1)}, u32[]{:S(2)}, u32[]{:S(2)}) collective-permute-start(bf16[264,1024]{1,0:T(8,128)(2,1)S(1)} %pad_maximum_fusion.refs_0_), channel_id=1, source_target_pairs={{0,16},{8,24},{16,32},{24,40},{32,48},{40,56},{48,0},{56,8},{64,80... | collective-permute-start | bytes 1622024 | tf_op jit(solution)/shard_map/ppermute | solution.py:54
  8.9 15.1 %collective-permute-start.8 = (bf16[264,1024]{1,0:T(8,128)(2,1)S(1)}, bf16[264,1024]{1,0:T(8,128)(2,1)S(1)}, u32[]{:S(2)}, u32[]{:S(2)}) collective-permute-start(bf16[264,1024]{1,0:T(8,128)(2,1)S(1)} %pad_maximum_fusion.refs_0_), channel_id=1, source_target_pairs={{0,64},{8,72},{16,80},{24,88},{32,96},{40,104},{48,112},{56,120},{... | collective-permute-start | bytes 1622024 | tf_op jit(solution)/shard_map/ppermute | solution.py:54
  16.6 90.4 %copy-start.5 = (bf16[264,1024]{1,0:T(8,128)(2,1)}, bf16[264,1024]{1,0:T(8,128)(2,1)S(1)}, u32[]{:S(2)}) copy-start(bf16[264,1024]{1,0:T(8,128)(2,1)S(1)} %collective-permute-done.1.refs_2_) | copy-start | bytes 1622020
  16.6 15.4 %collective-permute-start.12 = (bf16[264,1024]{1,0:T(8,128)(2,1)S(1)}, bf16[264,1024]{1,0:T(8,128)(2,1)S(1)}, u32[]{:S(2)}, u32[]{:S(2)}) collective-permute-start(bf16[264,1024]{1,0:T(8,128)(2,1)S(1)} %pad_maximum_fusion.refs_0_), channel_id=1, source_target_pairs={{0,48},{8,56},{16,0},{24,8},{32,16},{40,24},{48,32},{56,40},{64,11... | collective-permute-start | bytes 1622024 | tf_op jit(solution)/shard_map/ppermute | solution.py:54
  20.3 86.6 %copy-start.6 = (bf16[264,1024]{1,0:T(8,128)(2,1)}, bf16[264,1024]{1,0:T(8,128)(2,1)S(1)}, u32[]{:S(2)}) copy-start(bf16[264,1024]{1,0:T(8,128)(2,1)S(1)} %collective-permute-done.refs_1_) | copy-start | bytes 1622020
  20.3 14.7 %collective-permute-start.21 = (bf16[264,1024]{1,0:T(8,128)(2,1)S(1)}, bf16[264,1024]{1,0:T(8,128)(2,1)S(1)}, u32[]{:S(2)}, u32[]{:S(2)}) collective-permute-start(bf16[264,1024]{1,0:T(8,128)(2,1)S(1)} %pad_maximum_fusion.refs_0_), channel_id=1, source_target_pairs={{0,8},{8,0},{16,24},{24,16},{32,40},{40,32},{48,56},{56,48},{64,72... | collective-permute-start | bytes 1622024 | tf_op jit(solution)/shard_map/ppermute | solution.py:58
  20.3 63.8 %copy-start.9 = (bf16[264,1024]{1,0:T(8,128)(2,1)}, bf16[264,1024]{1,0:T(8,128)(2,1)S(1)}, u32[]{:S(2)}) copy-start(bf16[264,1024]{1,0:T(8,128)(2,1)S(1)} %collective-permute-done.16.refs_16_) | copy-start | bytes 1622020
  20.3 15.9 %collective-permute-start.3 = (bf16[264,1024]{1,0:T(8,128)(2,1)S(1)}, bf16[264,1024]{1,0:T(8,128)(2,1)S(1)}, u32[]{:S(2)}, u32[]{:S(2)}) collective-permute-start(bf16[264,1024]{1,0:T(8,128)(2,1)S(1)} %collective-permute-done.1.refs_2_), channel_id=1, source_target_pairs={{0,7},{1,0},{2,1},{3,2},{4,3},{5,4},{6,5},{7,6},{8,15},{9,8},{10,9... | collective-permute-start | bytes 1622024 | tf_op jit(solution)/shard_map/ppermute | solution.py:62
  23.4 60.8 %copy-start.10 = (bf16[264,1024]{1,0:T(8,128)(2,1)}, bf16[264,1024]{1,0:T(8,128)(2,1)S(1)}, u32[]{:S(2)}) copy-start(bf16[264,1024]{1,0:T(8,128)(2,1)S(1)} %collective-permute-done.22.refs_10_) | copy-start | bytes 1622020
  23.4 15.6 %collective-permute-start.2 = (bf16[264,1024]{1,0:T(8,128)(2,1)S(1)}, bf16[264,1024]{1,0:T(8,128)(2,1)S(1)}, u32[]{:S(2)}, u32[]{:S(2)}) collective-permute-start(bf16[264,1024]{1,0:T(8,128)(2,1)S(1)} %collective-permute-done.refs_1_), channel_id=1, source_target_pairs={{0,1},{1,2},{2,3},{3,4},{4,5},{5,6},{6,7},{7,0},{8,9},{9,10},{10,1... | collective-permute-start | bytes 1622024 | tf_op jit(solution)/shard_map/ppermute | solution.py:62
  24.0 60.2 %copy-start.11 = (bf16[264,1024]{1,0:T(8,128)(2,1)}, bf16[264,1024]{1,0:T(8,128)(2,1)S(1)}, u32[]{:S(2)}) copy-start(bf16[264,1024]{1,0:T(8,128)(2,1)S(1)} %collective-permute-done.8.refs_14_) | copy-start | bytes 1622020
  24.0 17.8 %collective-permute-start.17 = (bf16[264,1024]{1,0:T(8,128)(2,1)S(1)}, bf16[264,1024]{1,0:T(8,128)(2,1)S(1)}, u32[]{:S(2)}, u32[]{:S(2)}) collective-permute-start(bf16[264,1024]{1,0:T(8,128)(2,1)S(1)} %collective-permute-done.16.refs_16_), channel_id=1, source_target_pairs={{0,48},{8,56},{16,0},{24,8},{32,16},{40,24},{48,32},{56,40},{64,11... | collective-permute-start | bytes 1622024 | tf_op jit(solution)/shard_map/ppermute | solution.py:54
  32.0 52.2 %copy-start.12 = (bf16[264,1024]{1,0:T(8,128)(2,1)}, bf16[264,1024]{1,0:T(8,128)(2,1)S(1)}, u32[]{:S(2)}) copy-start(bf16[264,1024]{1,0:T(8,128)(2,1)S(1)} %collective-permute-done.12.refs_12_) | copy-start | bytes 1622020
  32.0 11.4 %collective-permute-start.30 = (bf16[264,1024]{1,0:T(8,128)(2,1)S(1)}, bf16[264,1024]{1,0:T(8,128)(2,1)S(1)}, u32[]{:S(2)}, u32[]{:S(2)}) collective-permute-start(bf16[264,1024]{1,0:T(8,128)(2,1)S(1)} %collective-permute-done.22.refs_10_), channel_id=1, source_target_pairs={{0,192},{8,200},{16,208},{24,216},{32,224},{40,232},{48,240},{56,2... | collective-permute-start | bytes 1622024 | tf_op jit(solution)/shard_map/ppermute | solution.py:54
  35.0 49.2 %copy-start.13 = (bf16[264,1024]{1,0:T(8,128)(2,1)}, bf16[264,1024]{1,0:T(8,128)(2,1)S(1)}, u32[]{:S(2)}) copy-start(bf16[264,1024]{1,0:T(8,128)(2,1)S(1)} %collective-permute-done.21.refs_9_) | copy-start | bytes 1622020
  35.0 16.8 %collective-permute-start.9 = (bf16[264,1024]{1,0:T(8,128)(2,1)S(1)}, bf16[264,1024]{1,0:T(8,128)(2,1)S(1)}, u32[]{:S(2)}, u32[]{:S(2)}) collective-permute-start(bf16[264,1024]{1,0:T(8,128)(2,1)S(1)} %collective-permute-done.8.refs_14_), channel_id=1, source_target_pairs={{0,16},{8,24},{16,32},{24,40},{32,48},{40,56},{48,0},{56,8},{64,80... | collective-permute-start | bytes 1622024 | tf_op jit(solution)/shard_map/ppermute | solution.py:54
  36.2 48.0 %copy-start.7 = (bf16[264,1024]{1,0:T(8,128)(2,1)}, bf16[264,1024]{1,0:T(8,128)(2,1)S(1)}, u32[]{:S(2)}) copy-start(bf16[264,1024]{1,0:T(8,128)(2,1)S(1)} %collective-permute-done.3.refs_4_) | copy-start | bytes 1622020
  36.2 16.4 %collective-permute-start.13 = (bf16[264,1024]{1,0:T(8,128)(2,1)S(1)}, bf16[264,1024]{1,0:T(8,128)(2,1)S(1)}, u32[]{:S(2)}, u32[]{:S(2)}) collective-permute-start(bf16[264,1024]{1,0:T(8,128)(2,1)S(1)} %collective-permute-done.12.refs_12_), channel_id=1, source_target_pairs={{0,64},{8,72},{16,80},{24,88},{32,96},{40,104},{48,112},{56,120},{... | collective-permute-start | bytes 1622024 | tf_op jit(solution)/shard_map/ppermute | solution.py:54
  39.0 19.9 %collective-permute-start.32 = (bf16[264,1024]{1,0:T(8,128)(2,1)S(1)}, bf16[264,1024]{1,0:T(8,128)(2,1)S(1)}, u32[]{:S(2)}, u32[]{:S(2)}) collective-permute-start(bf16[264,1024]{1,0:T(8,128)(2,1)S(1)} %collective-permute-done.22.refs_10_), channel_id=1, source_target_pairs={{0,16},{8,24},{16,32},{24,40},{32,48},{40,56},{48,0},{56,8},{64,80... | collective-permute-start | bytes 1622024 | tf_op jit(solution)/shard_map/ppermute | solution.py:54
  41.8 20.3 %collective-permute-start.35 = (bf16[264,1024]{1,0:T(8,128)(2,1)S(1)}, bf16[264,1024]{1,0:T(8,128)(2,1)S(1)}, u32[]{:S(2)}, u32[]{:S(2)}) collective-permute-start(bf16[264,1024]{1,0:T(8,128)(2,1)S(1)} %collective-permute-done.8.refs_14_), channel_id=1, source_target_pairs={{0,64},{8,72},{16,80},{24,88},{32,96},{40,104},{48,112},{56,120},{... | collective-permute-start | bytes 1622024 | tf_op jit(solution)/shard_map/ppermute | solution.py:54
  43.3 21.8 %collective-permute-start.23 = (bf16[264,1024]{1,0:T(8,128)(2,1)S(1)}, bf16[264,1024]{1,0:T(8,128)(2,1)S(1)}, u32[]{:S(2)}, u32[]{:S(2)}) collective-permute-start(bf16[264,1024]{1,0:T(8,128)(2,1)S(1)} %collective-permute-done.22.refs_10_), channel_id=1, source_target_pairs={{0,8},{8,0},{16,24},{24,16},{32,40},{40,32},{48,56},{56,48},{64,72... | collective-permute-start | bytes 1622024 | tf_op jit(solution)/shard_map/ppermute | solution.py:58
  51.8 13.3 %collective-permute-start.25 = (bf16[264,1024]{1,0:T(8,128)(2,1)S(1)}, bf16[264,1024]{1,0:T(8,128)(2,1)S(1)}, u32[]{:S(2)}, u32[]{:S(2)}) collective-permute-start(bf16[264,1024]{1,0:T(8,128)(2,1)S(1)} %collective-permute-done.8.refs_14_), channel_id=1, source_target_pairs={{0,8},{8,0},{16,24},{24,16},{32,40},{40,32},{48,56},{56,48},{64,72... | collective-permute-start | bytes 1622024 | tf_op jit(solution)/shard_map/ppermute | solution.py:58
  52.6 14.9 %collective-permute-start.24 = (bf16[264,1024]{1,0:T(8,128)(2,1)S(1)}, bf16[264,1024]{1,0:T(8,128)(2,1)S(1)}, u32[]{:S(2)}, u32[]{:S(2)}) collective-permute-start(bf16[264,1024]{1,0:T(8,128)(2,1)S(1)} %collective-permute-done.12.refs_12_), channel_id=1, source_target_pairs={{0,8},{8,0},{16,24},{24,16},{32,40},{40,32},{48,56},{56,48},{64,72... | collective-permute-start | bytes 1622024 | tf_op jit(solution)/shard_map/ppermute | solution.py:58
  58.9 10.3 %collective-permute-start.26 = (bf16[264,1024]{1,0:T(8,128)(2,1)S(1)}, bf16[264,1024]{1,0:T(8,128)(2,1)S(1)}, u32[]{:S(2)}, u32[]{:S(2)}) collective-permute-start(bf16[264,1024]{1,0:T(8,128)(2,1)S(1)} %collective-permute-done.16.refs_16_), channel_id=1, source_target_pairs={{0,8},{8,0},{16,24},{24,16},{32,40},{40,32},{48,56},{56,48},{64,72... | collective-permute-start | bytes 1622024 | tf_op jit(solution)/shard_map/ppermute | solution.py:58
  62.1 12.8 %collective-permute-start.5 = (bf16[264,1024]{1,0:T(8,128)(2,1)S(1)}, bf16[264,1024]{1,0:T(8,128)(2,1)S(1)}, u32[]{:S(2)}, u32[]{:S(2)}) collective-permute-start(bf16[264,1024]{1,0:T(8,128)(2,1)S(1)} %collective-permute-done.3.refs_4_), channel_id=1, source_target_pairs={{0,7},{1,0},{2,1},{3,2},{4,3},{5,4},{6,5},{7,6},{8,15},{9,8},{10,9... | collective-permute-start | bytes 1622024 | tf_op jit(solution)/shard_map/ppermute | solution.py:62
  65.1 13.6 %collective-permute-start.4 = (bf16[264,1024]{1,0:T(8,128)(2,1)S(1)}, bf16[264,1024]{1,0:T(8,128)(2,1)S(1)}, u32[]{:S(2)}, u32[]{:S(2)}) collective-permute-start(bf16[264,1024]{1,0:T(8,128)(2,1)S(1)} %collective-permute-done.2.refs_3_), channel_id=1, source_target_pairs={{0,1},{1,2},{2,3},{3,4},{4,5},{5,6},{6,7},{7,0},{8,9},{9,10},{10,1... | collective-permute-start | bytes 1622024 | tf_op jit(solution)/shard_map/ppermute | solution.py:62
  65.2 13.6 %collective-permute-start.18 = (bf16[264,1024]{1,0:T(8,128)(2,1)S(1)}, bf16[264,1024]{1,0:T(8,128)(2,1)}, u32[]{:S(2)}, u32[]{:S(2)}) collective-permute-start(bf16[264,1024]{1,0:T(8,128)(2,1)S(1)} %collective-permute-done.17.refs_20_), channel_id=1, source_target_pairs={{0,48},{8,56},{16,0},{24,8},{32,16},{40,24},{48,32},{56,40},{64,11... | collective-permute-start | bytes 1622024 | tf_op jit(solution)/shard_map/ppermute | solution.py:54
  67.4 11.8 %collective-permute-start.37 = (bf16[264,1024]{1,0:T(8,128)(2,1)S(1)}, bf16[264,1024]{1,0:T(8,128)(2,1)}, u32[]{:S(2)}, u32[]{:S(2)}) collective-permute-start(bf16[264,1024]{1,0:T(8,128)(2,1)S(1)} %collective-permute-done.30.refs_24_), channel_id=1, source_target_pairs={{0,192},{8,200},{16,208},{24,216},{32,224},{40,232},{48,240},{56,2... | collective-permute-start | bytes 1622024 | tf_op jit(solution)/shard_map/ppermute | solution.py:54
  69.2 10.2 %collective-permute-start.27 = (bf16[264,1024]{1,0:T(8,128)(2,1)S(1)}, bf16[264,1024]{1,0:T(8,128)(2,1)S(1)}, u32[]{:S(2)}, u32[]{:S(2)}) collective-permute-start(bf16[264,1024]{1,0:T(8,128)(2,1)S(1)} %collective-permute-done.9.refs_18_), channel_id=1, source_target_pairs={{0,8},{8,0},{16,24},{24,16},{32,40},{40,32},{48,56},{56,48},{64,72... | collective-permute-start | bytes 1622024 | tf_op jit(solution)/shard_map/ppermute | solution.py:58
  74.9 4.9 %collective-permute-start.31 = (bf16[264,1024]{1,0:T(8,128)(2,1)S(1)}, bf16[264,1024]{1,0:T(8,128)(2,1)S(1)}, u32[]{:S(2)}, u32[]{:S(2)}) collective-permute-start(bf16[264,1024]{1,0:T(8,128)(2,1)S(1)} %collective-permute-done.30.refs_24_), channel_id=1, source_target_pairs={{0,8},{8,0},{16,24},{24,16},{32,40},{40,32},{48,56},{56,48},{64,72... | collective-permute-start | bytes 1622024 | tf_op jit(solution)/shard_map/ppermute | solution.py:58
  78.8 1.9 %collective-permute-start.28 = (bf16[264,1024]{1,0:T(8,128)(2,1)S(1)}, bf16[264,1024]{1,0:T(8,128)(2,1)S(1)}, u32[]{:S(2)}, u32[]{:S(2)}) collective-permute-start(bf16[264,1024]{1,0:T(8,128)(2,1)S(1)} %collective-permute-done.17.refs_20_), channel_id=1, source_target_pairs={{0,8},{8,0},{16,24},{24,16},{32,40},{40,32},{48,56},{56,48},{64,72... | collective-permute-start | bytes 1622024 | tf_op jit(solution)/shard_map/ppermute | solution.py:58
  78.8 3.2 %collective-permute-start.29 = (bf16[264,1024]{1,0:T(8,128)(2,1)S(1)}, bf16[264,1024]{1,0:T(8,128)(2,1)S(1)}, u32[]{:S(2)}, u32[]{:S(2)}) collective-permute-start(bf16[264,1024]{1,0:T(8,128)(2,1)S(1)} %collective-permute-done.13.refs_22_), channel_id=1, source_target_pairs={{0,8},{8,0},{16,24},{24,16},{32,40},{40,32},{48,56},{56,48},{64,72... | collective-permute-start | bytes 1622024 | tf_op jit(solution)/shard_map/ppermute | solution.py:58
  79.3 4.9 %collective-permute-start.33 = (bf16[264,1024]{1,0:T(8,128)(2,1)S(1)}, bf16[264,1024]{1,0:T(8,128)(2,1)S(1)}, u32[]{:S(2)}, u32[]{:S(2)}) collective-permute-start(bf16[264,1024]{1,0:T(8,128)(2,1)S(1)} %collective-permute-done.32.refs_26_), channel_id=1, source_target_pairs={{0,8},{8,0},{16,24},{24,16},{32,40},{40,32},{48,56},{56,48},{64,72... | collective-permute-start | bytes 1622024 | tf_op jit(solution)/shard_map/ppermute | solution.py:58
  79.4 4.8 %collective-permute-start.36 = (bf16[264,1024]{1,0:T(8,128)(2,1)S(1)}, bf16[264,1024]{1,0:T(8,128)(2,1)S(1)}, u32[]{:S(2)}, u32[]{:S(2)}) collective-permute-start(bf16[264,1024]{1,0:T(8,128)(2,1)S(1)} %collective-permute-done.35.refs_30_), channel_id=1, source_target_pairs={{0,8},{8,0},{16,24},{24,16},{32,40},{40,32},{48,56},{56,48},{64,72... | collective-permute-start | bytes 1622024 | tf_op jit(solution)/shard_map/ppermute | solution.py:58
  79.8 15.6 %collective-permute-start.10 = (bf16[264,1024]{1,0:T(8,128)(2,1)S(1)}, bf16[264,1024]{1,0:T(8,128)(2,1)}, u32[]{:S(2)}, u32[]{:S(2)}) collective-permute-start(bf16[264,1024]{1,0:T(8,128)(2,1)S(1)} %collective-permute-done.9.refs_18_), channel_id=1, source_target_pairs={{0,16},{8,24},{16,32},{24,40},{32,48},{40,56},{48,0},{56,8},{64,80... | collective-permute-start | bytes 1622024 | tf_op jit(solution)/shard_map/ppermute | solution.py:54
  80.7 17.7 %collective-permute-start.14 = (bf16[264,1024]{1,0:T(8,128)(2,1)S(1)}, bf16[264,1024]{1,0:T(8,128)(2,1)}, u32[]{:S(2)}, u32[]{:S(2)}) collective-permute-start(bf16[264,1024]{1,0:T(8,128)(2,1)S(1)} %collective-permute-done.13.refs_22_), channel_id=1, source_target_pairs={{0,64},{8,72},{16,80},{24,88},{32,96},{40,104},{48,112},{56,120},{... | collective-permute-start | bytes 1622024 | tf_op jit(solution)/shard_map/ppermute | solution.py:54
  81.9 24.9 %collective-permute-start.19 = (bf16[264,1024]{1,0:T(8,128)(2,1)}, bf16[264,1024]{1,0:T(8,128)(2,1)}, u32[]{:S(2)}, u32[]{:S(2)}) collective-permute-start(bf16[264,1024]{1,0:T(8,128)(2,1)} %collective-permute-done.18.refs_28_), channel_id=1, source_target_pairs={{0,192},{8,200},{16,208},{24,216},{32,224},{40,232},{48,240},{56,2... | collective-permute-start | bytes 1622024 | tf_op jit(solution)/shard_map/ppermute | solution.py:54
  84.2 22.8 %collective-permute-start.34 = (bf16[264,1024]{1,0:T(8,128)(2,1)}, bf16[264,1024]{1,0:T(8,128)(2,1)}, u32[]{:S(2)}, u32[]{:S(2)}) collective-permute-start(bf16[264,1024]{1,0:T(8,128)(2,1)} %collective-permute-done.18.refs_28_), channel_id=1, source_target_pairs={{0,8},{8,0},{16,24},{24,16},{32,40},{40,32},{48,56},{56,48},{64,72... | collective-permute-start | bytes 1622024 | tf_op jit(solution)/shard_map/ppermute | solution.py:58
  85.0 22.0 %collective-permute-start.38 = (bf16[264,1024]{1,0:T(8,128)(2,1)}, bf16[264,1024]{1,0:T(8,128)(2,1)}, u32[]{:S(2)}, u32[]{:S(2)}) collective-permute-start(bf16[264,1024]{1,0:T(8,128)(2,1)} %collective-permute-done.37.refs_32_), channel_id=1, source_target_pairs={{0,8},{8,0},{16,24},{24,16},{32,40},{40,32},{48,56},{56,48},{64,72... | collective-permute-start | bytes 1622024 | tf_op jit(solution)/shard_map/ppermute | solution.py:58
  95.4 10.9 %collective-permute-start.7 = (bf16[136,1024]{1,0:T(8,128)(2,1)S(1)}, bf16[136,1024]{1,0:T(8,128)(2,1)S(1)}, u32[]{:S(2)}, u32[]{:S(2)}) collective-permute-start(bf16[136,1024]{1,0:T(8,128)(2,1)S(1)} %slice.9), channel_id=1, source_target_pairs={{0,7},{1,0},{2,1},{3,2},{4,3},{5,4},{6,5},{7,6},{8,15},{9,8},{10,9... | collective-permute-start | bytes 835592 | tf_op jit(solution)/shard_map/ppermute | solution.py:62
  98.4 7.9 %collective-permute-start.6 = (bf16[128,1024]{1,0:T(8,128)(2,1)S(1)}, bf16[128,1024]{1,0:T(8,128)(2,1)}, u32[]{:S(2)}, u32[]{:S(2)}) collective-permute-start(bf16[128,1024]{1,0:T(8,128)(2,1)S(1)} %slice.8), channel_id=1, source_target_pairs={{0,1},{1,2},{2,3},{3,4},{4,5},{5,6},{6,7},{7,0},{8,9},{9,10},{10,1... | collective-permute-start | bytes 786440 | tf_op jit(solution)/shard_map/ppermute | solution.py:62
  106.3 27.5 %collective-permute-start.11 = (bf16[264,1024]{1,0:T(8,128)(2,1)}, bf16[264,1024]{1,0:T(8,128)(2,1)S(1)}, u32[]{:S(2)}, u32[]{:S(2)}) collective-permute-start(bf16[264,1024]{1,0:T(8,128)(2,1)} %collective-permute-done.10.refs_9_), channel_id=1, source_target_pairs={{0,8},{8,0},{16,24},{24,16},{32,40},{40,32},{48,56},{56,48},{64,72... | collective-permute-start | bytes 1622024 | tf_op jit(solution)/shard_map/ppermute | solution.py:58
  106.3 27.5 %collective-permute-start.15 = (bf16[264,1024]{1,0:T(8,128)(2,1)}, bf16[264,1024]{1,0:T(8,128)(2,1)S(1)}, u32[]{:S(2)}, u32[]{:S(2)}) collective-permute-start(bf16[264,1024]{1,0:T(8,128)(2,1)} %collective-permute-done.14.refs_11_), channel_id=1, source_target_pairs={{0,8},{8,0},{16,24},{24,16},{32,40},{40,32},{48,56},{56,48},{64,72... | collective-permute-start | bytes 1622024 | tf_op jit(solution)/shard_map/ppermute | solution.py:58
  106.8 27.0 %collective-permute-start.20 = (bf16[264,1024]{1,0:T(8,128)(2,1)}, bf16[264,1024]{1,0:T(8,128)(2,1)S(1)}, u32[]{:S(2)}, u32[]{:S(2)}) collective-permute-start(bf16[264,1024]{1,0:T(8,128)(2,1)} %collective-permute-done.19.refs_13_), channel_id=1, source_target_pairs={{0,8},{8,0},{16,24},{24,16},{32,40},{40,32},{48,56},{56,48},{64,72... | collective-permute-start | bytes 1622024 | tf_op jit(solution)/shard_map/ppermute | solution.py:58
  (26 other events, 426.8 us)
